TPU v7x, 512 devices: a whole 4x4x16 slice. The times are simulated.
512 devices in a mesh: seq: 128 (over y, z, core), ch: 4 (over x).
Axes of the slice: x: 4, y: 4, z: 16, core: 2. Of those that a mesh axis runs over, the one named last changes fastest.
Arguments:
- qkv: bfloat16 [3, 16384, 2048], P(None, 'seq', 'ch'), may hold values from -6 to 6
- filt: float32 [16384, 2048], P('seq', 'ch'), may hold values from -0.1875 to 0.1875
- skip_gain: float32 [2048], P('ch'), may hold values from -4 to 4
- short_weight: float32 [3, 3, 2048], P(None, None, 'ch'), may hold values from -3.5 to 3.5
- w_out: bfloat16 [2048, 2048], P(None, 'ch'), may hold values from -0.125 to 0.125
- g_out: bfloat16 [16384, 2048], P('seq', 'ch'), may hold values from -6 to 6
Outputs:
- output: bfloat16 [16384, 2048], P('seq', 'ch')
- grad_qkv: bfloat16 [3, 16384, 2048], P(None, 'seq', 'ch')
- grad_filter: float32 [16384, 2048], P('seq', 'ch')
All inputs are finite; a program needn't handle non-finite values.
Results may differ from a plain program's by a relative error of at most 0.0049.
Values may be sent and summed in bfloat16 or wider, within the bound.
A program may use at most 64 MiB of HBM per device.

v0:
```python
import math

import jax
import jax.numpy as jnp
from jax import lax
from jax.sharding import PartitionSpec as P

HIGHEST = lax.Precision.HIGHEST
TWO_PI = 2.0 * math.pi


def passed_along(block, axis, distance):
    devices = range(lax.axis_size(axis))
    route = [(i - distance, i) for i in devices if i - distance in devices]
    return lax.ppermute(block, axis, route)


def phase_pair(left_count, right_count, period, left_start, right_start):
    left_idx = lax.broadcasted_iota(jnp.int32, (left_count, right_count), 0) + left_start
    right_idx = lax.broadcasted_iota(jnp.int32, (left_count, right_count), 1) + right_start
    angle_all = (left_idx * right_idx % period).astype(jnp.float32) * (TWO_PI / period)
    return (jnp.cos(angle_all), jnp.sin(angle_all))


def contract(pattern, matrix, values):
    return jnp.einsum(
        pattern, matrix, values, precision=HIGHEST, preferred_element_type=jnp.float32
    )


def forward_spectrum(signal):
    seq_parts = lax.axis_size("seq")
    row_count = signal.shape[0]
    row_share = row_count // seq_parts
    period = 2 * seq_parts * row_count
    spread_in = lax.all_to_all(signal[None], "seq", split_axis=1, concat_axis=0, tiled=True)
    outer_cos, outer_sin = phase_pair(2 * seq_parts, seq_parts, 2 * seq_parts, 0, 0)
    section_re = contract("cp,prw->crw", outer_cos, spread_in)
    section_im = -contract("cp,prw->crw", outer_sin, spread_in)
    twist_cos, twist_sin = phase_pair(
        2 * seq_parts, row_share, period, 0, lax.axis_index("seq") * row_share
    )
    twist_cos = twist_cos[:, :, None]
    twist_sin = twist_sin[:, :, None]
    turned_re = section_re * twist_cos + section_im * twist_sin
    turned_im = section_im * twist_cos - section_re * twist_sin
    inner_cos, inner_sin = phase_pair(row_count, row_count, row_count, 0, 0)
    piece_re = lax.all_to_all(turned_re, "seq", split_axis=0, concat_axis=1, tiled=True)
    piece_im = lax.all_to_all(turned_im, "seq", split_axis=0, concat_axis=1, tiled=True)
    spec_re = contract("dm,cmk->cdk", inner_cos, piece_re) + contract(
        "dm,cmk->cdk", inner_sin, piece_im
    )
    spec_im = contract("dm,cmk->cdk", inner_cos, piece_im) - contract(
        "dm,cmk->cdk", inner_sin, piece_re
    )
    return (spec_re, spec_im)


def time_signal(spec_re, spec_im):
    seq_parts = lax.axis_size("seq")
    row_count = spec_re.shape[1]
    period = 2 * seq_parts * row_count
    inner_cos, inner_sin = phase_pair(row_count, row_count, row_count, 0, 0)
    back_re = contract("md,cdk->cmk", inner_cos, spec_re) - contract(
        "md,cdk->cmk", inner_sin, spec_im
    )
    back_im = contract("md,cdk->cmk", inner_cos, spec_im) + contract(
        "md,cdk->cmk", inner_sin, spec_re
    )
    twist_cos, twist_sin = phase_pair(2, row_count, period, 2 * lax.axis_index("seq"), 0)
    twist_cos = twist_cos[:, :, None]
    twist_sin = twist_sin[:, :, None]
    turned_re = back_re * twist_cos - back_im * twist_sin
    turned_im = back_im * twist_cos + back_re * twist_sin
    outer_cos, outer_sin = phase_pair(seq_parts, 2 * seq_parts, 2 * seq_parts, 0, 0)
    piece_re = lax.all_to_all(turned_re, "seq", split_axis=1, concat_axis=0, tiled=True)
    piece_im = lax.all_to_all(turned_im, "seq", split_axis=1, concat_axis=0, tiled=True)
    summed = contract("pc,crk->prk", outer_cos, piece_re) - contract(
        "pc,crk->prk", outer_sin, piece_im
    )
    returned = summed * (1.0 / period)
    return lax.all_to_all(returned, "seq", split_axis=0, concat_axis=1, tiled=True)[0]


def local(qkv, filt, skip_gain, short_weight, w_out, g_out):
    row_count = qkv.shape[1]
    slab_width = qkv.shape[2]
    tail_rows = passed_along(qkv[:, row_count - 2 :, :], "seq", 1)
    extended = jnp.concatenate([tail_rows, qkv], axis=1)
    short = (
        short_weight[:, 0, None, :] * extended[:, 2:, :]
        + short_weight[:, 1, None, :] * extended[:, 1:-1, :]
        + short_weight[:, 2, None, :] * extended[:, :-2, :]
    )
    query_gate = short[0]
    key_short = short[1]
    value_short = short[2]
    mixed = key_short * value_short
    both_re, both_im = forward_spectrum(jnp.concatenate([mixed, filt], axis=1))
    signal_re = both_re[:, :, :slab_width]
    signal_im = both_im[:, :, :slab_width]
    kernel_re = both_re[:, :, slab_width:]
    kernel_im = both_im[:, :, slab_width:]
    conv_out = time_signal(
        signal_re * kernel_re - signal_im * kernel_im, signal_re * kernel_im + signal_im * kernel_re
    )
    long_out = conv_out + skip_gain * mixed
    gated_out = (query_gate * long_out).astype(jnp.bfloat16)
    projected = jnp.dot(
        lax.all_gather(gated_out, "ch", axis=1, tiled=True),
        w_out,
        preferred_element_type=jnp.float32,
    )
    output = projected.astype(jnp.bfloat16)
    grad_all = lax.all_gather(g_out, "ch", axis=1, tiled=True)
    rows_all = lax.all_to_all(w_out, "ch", split_axis=0, concat_axis=1, tiled=True)
    grad_gated = lax.dot_general(
        grad_all, rows_all, (((1,), (1,)), ((), ())), preferred_element_type=jnp.float32
    )
    grad_long = grad_gated * query_gate
    grad_query = grad_gated * long_out
    grad_re, grad_im = forward_spectrum(grad_long)
    pair_re = jnp.concatenate(
        [kernel_re * grad_re + kernel_im * grad_im, signal_re * grad_re + signal_im * grad_im],
        axis=2,
    )
    pair_im = jnp.concatenate(
        [kernel_re * grad_im - kernel_im * grad_re, signal_re * grad_im - signal_im * grad_re],
        axis=2,
    )
    pair_time = time_signal(pair_re, pair_im)
    grad_mixed = pair_time[:, :slab_width] + skip_gain * grad_long
    token_total = lax.axis_size("seq") * row_count
    grad_filter = pair_time[:, slab_width:] * (1.0 / math.sqrt(token_total))
    grad_short = jnp.stack([grad_query, grad_mixed * value_short, grad_mixed * key_short])
    head_rows = passed_along(grad_short[:, :2, :], "seq", -1)
    extended_grad = jnp.concatenate([grad_short, head_rows], axis=1)
    grad_qkv = (
        short_weight[:, 0, None, :] * extended_grad[:, :-2, :]
        + short_weight[:, 1, None, :] * extended_grad[:, 1:-1, :]
        + short_weight[:, 2, None, :] * extended_grad[:, 2:, :]
    ).astype(jnp.bfloat16)
    return (output, grad_qkv, grad_filter)


def solution(mesh):
    in_specs = (
        P(None, "seq", "ch"),
        P("seq", "ch"),
        P("ch"),
        P(None, None, "ch"),
        P(None, "ch"),
        P("seq", "ch"),
    )
    out_specs = (P("seq", "ch"), P(None, "seq", "ch"), P("seq", "ch"))
    return jax.shard_map(local, mesh=mesh, in_specs=in_specs, out_specs=out_specs, check_vma=False)
```

profile of v0, /device:TPU:1, one launch (start us, length us, event | category | flops | bytes accessed | tf_op | source)
XLA Modules:
  0.0 649.4 jit_solution(5705717059407092852)
XLA Ops:
  0.7 5.0 all-to-all-start.6
  6.4 4.4 collective-permute-start
  10.8 24.7 %all_gather.7 = bf16[128,2048]{1,0:T(8,128)(2,1)S(1)} all-gather(bf16[128,512]{1,0:T(8,128)(2,1)S(1)} %copy-done.18), channel_id=1, replica_groups=mesh['seq'=128,'ch'=4] {'ch'}, dimensions={1}, use_global_device_ids=true | all-gather | bytes 655360 | tf_op jit(solution)/shard_map/all_gather | solution.py:115
  35.5 1.6 multiply_add_fusion
  37.1 2.4 copy.51
  39.5 2.1 fusion.230
  42.7 24.8 %all-to-all-start.7 = ((f32[1,128,512]{2,0,1:T(1,128)}), f32[1,128,512]{2,0,1:T(1,128)S(1)}, u32[]{:S(2)}, u32[]{:S(2)}) async-start(f32[1,128,512]{2,0,1:T(1,128)} %copy.52), calls=%async_computation.7 | async-start | bytes 524288 | tf_op jit(solution)/shard_map/all_to_all | solution.py:36
  68.9 21.0 %all-to-all-done.7 = f32[1,128,512]{2,0,1:T(1,128)S(1)} async-done(((f32[1,128,512]{2,0,1:T(1,128)}), f32[1,128,512]{2,0,1:T(1,128)S(1)}, u32[]{:S(2)}, u32[]{:S(2)}) %all-to-all-start.7) | async-done | bytes 262176 | tf_op jit(solution)/shard_map/all_to_all | solution.py:36
  89.9 7.4 %all-to-all-start = ((f32[1,128,1024]{2,0,1:T(1,128)}), f32[1,128,1024]{2,0,1:T(1,128)S(1)}, u32[]{:S(2)}, u32[]{:S(2)}) async-start(f32[1,128,1024]{2,0,1:T(1,128)} %copy.43), calls=%async_computation | async-start | bytes 1048576 | tf_op jit(solution)/shard_map/all_to_all | solution.py:36
  100.9 29.7 %all-to-all-done = f32[1,128,1024]{2,0,1:T(1,128)S(1)} async-done(((f32[1,128,1024]{2,0,1:T(1,128)}), f32[1,128,1024]{2,0,1:T(1,128)S(1)}, u32[]{:S(2)}, u32[]{:S(2)}) %all-to-all-start) | async-done | bytes 524320 | tf_op jit(solution)/shard_map/all_to_all | solution.py:36
  130.6 7.1 %all-to-all-start.8 = ((f32[256,1,512]{2,1,0:T(1,128)}), f32[256,1,512]{2,1,0:T(1,128)S(1)}, u32[]{:S(2)}, u32[]{:S(2)}) async-start(f32[256,1,512]{2,1,0:T(1,128)} %copy.53), calls=%async_computation.8 | async-start | bytes 1048576 | tf_op jit(solution)/shard_map/all_to_all | solution.py:48
  139.1 31.9 %all-to-all-done.8 = f32[256,1,512]{2,1,0:T(1,128)S(1)} async-done(((f32[256,1,512]{2,1,0:T(1,128)}), f32[256,1,512]{2,1,0:T(1,128)S(1)}, u32[]{:S(2)}, u32[]{:S(2)}) %all-to-all-start.8) | async-done | bytes 524320 | tf_op jit(solution)/shard_map/all_to_all | solution.py:48
  170.9 7.6 %all-to-all-start.9 = ((f32[256,1,512]{2,1,0:T(1,128)}), f32[256,1,512]{2,1,0:T(1,128)S(1)}, u32[]{:S(2)}, u32[]{:S(2)}) async-start(f32[256,1,512]{2,1,0:T(1,128)} %copy.55), calls=%async_computation.9 | async-start | bytes 1048576 | tf_op jit(solution)/shard_map/all_to_all | solution.py:49
  178.5 1.5 convolution_negate_fusion
  180.0 1.7 add_bitcast_fusion.1
  181.7 2.1 copy.44
  183.8 27.9 %all-to-all-done.9 = f32[256,1,512]{2,1,0:T(1,128)S(1)} async-done(((f32[256,1,512]{2,1,0:T(1,128)}), f32[256,1,512]{2,1,0:T(1,128)S(1)}, u32[]{:S(2)}, u32[]{:S(2)}) %all-to-all-start.9) | async-done | bytes 524320 | tf_op jit(solution)/shard_map/all_to_all | solution.py:49
  211.7 7.6 %all-to-all-start.1 = ((f32[256,1,1024]{2,1,0:T(1,128)}), f32[256,1,1024]{2,1,0:T(1,128)}, u32[]{:S(2)}, u32[]{:S(2)}) async-start(f32[256,1,1024]{2,1,0:T(1,128)} %copy.44), calls=%async_computation.1 | async-start | bytes 2097152 | tf_op jit(solution)/shard_map/all_to_all | solution.py:48
  219.3 2.1 copy.46
  221.4 51.9 %all-to-all-done.1 = f32[256,1,1024]{2,1,0:T(1,128)} async-done(((f32[256,1,1024]{2,1,0:T(1,128)}), f32[256,1,1024]{2,1,0:T(1,128)}, u32[]{:S(2)}, u32[]{:S(2)}) %all-to-all-start.1) | async-done | bytes 1048608 | tf_op jit(solution)/shard_map/all_to_all | solution.py:48
  273.4 8.8 %all-to-all-start.2 = ((f32[256,1,1024]{2,1,0:T(1,128)}), f32[256,1,1024]{2,1,0:T(1,128)S(1)}, u32[]{:S(2)}, u32[]{:S(2)}) async-start(f32[256,1,1024]{2,1,0:T(1,128)} %copy.46), calls=%async_computation.2 | async-start | bytes 2097152 | tf_op jit(solution)/shard_map/all_to_all | solution.py:49
  284.0 1.6 fusion.25
  285.6 1.6 fusion.5
  287.2 2.3 copy.45
  289.6 2.2 fusion.9
  291.8 44.7 %all-to-all-done.2 = f32[256,1,1024]{2,1,0:T(1,128)S(1)} async-done(((f32[256,1,1024]{2,1,0:T(1,128)}), f32[256,1,1024]{2,1,0:T(1,128)S(1)}, u32[]{:S(2)}, u32[]{:S(2)}) %all-to-all-start.2) | async-done | bytes 1048608 | tf_op jit(solution)/shard_map/all_to_all | solution.py:49
  337.5 2.3 copy.47
  343.7 1.9 multiply_add_fusion.2
  348.1 1.9 add_bitcast_fusion.3
  349.9 2.0 copy.48
  352.0 9.4 %all-to-all-start.3 = ((f32[2,128,512]{2,0,1:T(2,128)}), f32[2,128,512]{2,0,1:T(2,128)}, u32[]{:S(2)}, u32[]{:S(2)}) async-start(f32[2,128,512]{2,0,1:T(2,128)} %copy.48), calls=%async_computation.3 | async-start | bytes 1048576 | tf_op jit(solution)/shard_map/all_to_all | solution.py:76
  365.1 2.4 add_bitcast_fusion
  367.5 2.3 copy.57
  369.7 24.3 %all-to-all-done.3 = f32[2,128,512]{2,0,1:T(2,128)} async-done(((f32[2,128,512]{2,0,1:T(2,128)}), f32[2,128,512]{2,0,1:T(2,128)}, u32[]{:S(2)}, u32[]{:S(2)}) %all-to-all-start.3) | async-done | bytes 524320 | tf_op jit(solution)/shard_map/all_to_all | solution.py:76
  394.1 7.1 %all-to-all-start.10 = ((f32[2,128,1024]{2,0,1:T(2,128)}), f32[2,128,1024]{2,0,1:T(2,128)S(1)}, u32[]{:S(2)}, u32[]{:S(2)}) async-start(f32[2,128,1024]{2,0,1:T(2,128)} %copy.57), calls=%async_computation.10 | async-start | bytes 2097152 | tf_op jit(solution)/shard_map/all_to_all | solution.py:76
  402.5 53.1 %all-to-all-done.10 = f32[2,128,1024]{2,0,1:T(2,128)S(1)} async-done(((f32[2,128,1024]{2,0,1:T(2,128)}), f32[2,128,1024]{2,0,1:T(2,128)S(1)}, u32[]{:S(2)}, u32[]{:S(2)}) %all-to-all-start.10) | async-done | bytes 1048608 | tf_op jit(solution)/shard_map/all_to_all | solution.py:76
  455.6 8.4 %all-to-all-start.11 = ((f32[2,128,1024]{2,0,1:T(2,128)}), f32[2,128,1024]{2,0,1:T(2,128)S(1)}, u32[]{:S(2)}, u32[]{:S(2)}) async-start(f32[2,128,1024]{2,0,1:T(2,128)} %copy.58), calls=%async_computation.11 | async-start | bytes 2097152 | tf_op jit(solution)/shard_map/all_to_all | solution.py:77
  465.0 53.4 %all-to-all-done.11 = f32[2,128,1024]{2,0,1:T(2,128)S(1)} async-done(((f32[2,128,1024]{2,0,1:T(2,128)}), f32[2,128,1024]{2,0,1:T(2,128)S(1)}, u32[]{:S(2)}, u32[]{:S(2)}) %all-to-all-start.11) | async-done | bytes 1048608 | tf_op jit(solution)/shard_map/all_to_all | solution.py:77
  518.4 8.7 %all-to-all-start.4 = ((f32[2,128,512]{2,0,1:T(2,128)}), f32[2,128,512]{2,0,1:T(2,128)S(1)}, u32[]{:S(2)}, u32[]{:S(2)}) async-start(f32[2,128,512]{2,0,1:T(2,128)} %copy.49), calls=%async_computation.4 | async-start | bytes 1048576 | tf_op jit(solution)/shard_map/all_to_all | solution.py:77
  527.1 1.7 reshape.170
  528.8 1.7 reshape.171
  534.3 25.9 %all-to-all-done.4 = f32[2,128,512]{2,0,1:T(2,128)S(1)} async-done(((f32[2,128,512]{2,0,1:T(2,128)}), f32[2,128,512]{2,0,1:T(2,128)S(1)}, u32[]{:S(2)}, u32[]{:S(2)}) %all-to-all-start.4) | async-done | bytes 524320 | tf_op jit(solution)/shard_map/all_to_all | solution.py:77
  560.2 7.1 %all-to-all-start.12 = ((f32[128,1,1024]{2,1,0:T(1,128)}), f32[128,1,1024]{2,1,0:T(1,128)S(1)}, u32[]{:S(2)}, u32[]{:S(2)}) async-start(f32[128,1,1024]{2,1,0:T(1,128)} %copy.59), calls=%async_computation.12 | async-start | bytes 1048576 | tf_op jit(solution)/shard_map/all_to_all | solution.py:82
  572.0 28.5 %all-to-all-done.12 = f32[128,1,1024]{2,1,0:T(1,128)S(1)} async-done(((f32[128,1,1024]{2,1,0:T(1,128)}), f32[128,1,1024]{2,1,0:T(1,128)S(1)}, u32[]{:S(2)}, u32[]{:S(2)}) %all-to-all-start.12) | async-done | bytes 524320 | tf_op jit(solution)/shard_map/all_to_all | solution.py:82
  600.5 7.1 %all-to-all-start.5 = ((f32[128,1,512]{2,1,0:T(1,128)}), f32[128,1,512]{2,1,0:T(1,128)S(1)}, u32[]{:S(2)}, u32[]{:S(2)}) async-start(f32[128,1,512]{2,1,0:T(1,128)} %copy.50), calls=%async_computation.5 | async-start | bytes 524288 | tf_op jit(solution)/shard_map/all_to_all | solution.py:82
  607.8 22.3 %all-to-all-done.5 = f32[128,1,512]{2,1,0:T(1,128)S(1)} async-done(((f32[128,1,512]{2,1,0:T(1,128)}), f32[128,1,512]{2,1,0:T(1,128)S(1)}, u32[]{:S(2)}, u32[]{:S(2)}) %all-to-all-start.5) | async-done | bytes 262176 | tf_op jit(solution)/shard_map/all_to_all | solution.py:82
  631.1 4.3 collective-permute-start.1
  635.4 11.6 %all_gather.6 = bf16[128,2048]{1,0:T(8,128)(2,1)S(1)} all-gather(bf16[128,512]{1,0:T(8,128)(2,1)S(1)} %get-tuple-element.19), channel_id=1, replica_groups=mesh['seq'=128,'ch'=4] {'ch'}, dimensions={1}, use_global_device_ids=true | all-gather | bytes 655360 | tf_op jit(solution)/shard_map/all_gather | solution.py:110
  (90 shorter events, 34.9 us)
Async XLA Ops:
  0.6 10.1 %copy-start.19 = (f32[3,3,512]{2,1,0:T(4,128)S(1)}, f32[3,3,512]{2,1,0:T(4,128)}, u32[]{:S(2)}) copy-start(f32[3,3,512]{2,1,0:T(4,128)} %param.9) | copy-start | bytes 55300
  0.6 10.2 %copy-start.18 = (bf16[128,512]{1,0:T(8,128)(2,1)S(1)}, bf16[128,512]{1,0:T(8,128)(2,1)}, u32[]{:S(2)}) copy-start(bf16[128,512]{1,0:T(8,128)(2,1)} %param.11) | copy-start | bytes 393220
  0.7 36.4 %all-to-all-start.6 = ((bf16[4,512,512]{2,1,0:T(8,128)(2,1)}), bf16[4,512,512]{2,1,0:T(8,128)(2,1)S(1)}, u32[]{:S(2)}, u32[]{:S(2)}) async-start(bf16[4,512,512]{2,1,0:T(8,128)(2,1)} %bitcast.200), calls=%async_computation.6 | async-start | bytes 4194304 | tf_op jit(solution)/shard_map/all_to_all | solution.py:116
  6.4 29.1 %collective-permute-start = (bf16[3,2,512]{2,1,0:T(2,128)(2,1)S(1)}, bf16[3,2,512]{2,1,0:T(2,128)(2,1)S(1)}, u32[]{:S(2)}, u32[]{:S(2)}) collective-permute-start(bf16[3,2,512]{2,1,0:T(2,128)(2,1)S(1)} %slice.59), channel_id=1, source_target_pairs={{0,4},{4,8},{8,12},{12,16},{16,20},{20,24},{24,28},{28,32},{32,36}... | collective-permute-start | bytes 18440 | tf_op jit(solution)/shard_map/ppermute | solution.py:15
  39.5 28.0 %copy-start.17 = (f32[128,512]{1,0:T(8,128)S(1)}, f32[128,512]{1,0:T(8,128)}, u32[]{:S(2)}) copy-start(f32[128,512]{1,0:T(8,128)} %param.7) | copy-start | bytes 786436
  41.6 27.3 %copy-start.8 = (f32[128,512]{1,0:T(8,128)}, f32[128,512]{1,0:T(8,128)S(1)}, u32[]{:S(2)}) copy-start(f32[128,512]{1,0:T(8,128)S(1)} %fusion.230) | copy-start | bytes 786436
  41.7 48.2 %copy-start.6 = (f32[128,512]{1,0:T(8,128)}, f32[128,512]{1,0:T(8,128)S(1)}, u32[]{:S(2)}) copy-start(f32[128,512]{1,0:T(8,128)S(1)} %get-tuple-element.22) | copy-start | bytes 786436
  42.7 47.2 %all-to-all-start.7 = ((f32[1,128,512]{2,0,1:T(1,128)}), f32[1,128,512]{2,0,1:T(1,128)S(1)}, u32[]{:S(2)}, u32[]{:S(2)}) async-start(f32[1,128,512]{2,0,1:T(1,128)} %copy.52), calls=%async_computation.7 | async-start | bytes 524288 | tf_op jit(solution)/shard_map/all_to_all | solution.py:36
  89.9 40.7 %all-to-all-start = ((f32[1,128,1024]{2,0,1:T(1,128)}), f32[1,128,1024]{2,0,1:T(1,128)S(1)}, u32[]{:S(2)}, u32[]{:S(2)}) async-start(f32[1,128,1024]{2,0,1:T(1,128)} %copy.43), calls=%async_computation | async-start | bytes 1048576 | tf_op jit(solution)/shard_map/all_to_all | solution.py:36
  130.6 40.3 %all-to-all-start.8 = ((f32[256,1,512]{2,1,0:T(1,128)}), f32[256,1,512]{2,1,0:T(1,128)S(1)}, u32[]{:S(2)}, u32[]{:S(2)}) async-start(f32[256,1,512]{2,1,0:T(1,128)} %copy.53), calls=%async_computation.8 | async-start | bytes 1048576 | tf_op jit(solution)/shard_map/all_to_all | solution.py:48
  170.9 10.8 %copy-start.10 = (f32[256,1,512]{2,1,0:T(1,128)}, f32[256,1,512]{2,1,0:T(1,128)S(1)}, u32[]{:S(2)}) copy-start(f32[256,1,512]{2,1,0:T(1,128)S(1)} %all-to-all-done.8) | copy-start | bytes 1572868
  170.9 40.8 %all-to-all-start.9 = ((f32[256,1,512]{2,1,0:T(1,128)}), f32[256,1,512]{2,1,0:T(1,128)S(1)}, u32[]{:S(2)}, u32[]{:S(2)}) async-start(f32[256,1,512]{2,1,0:T(1,128)} %copy.55), calls=%async_computation.9 | async-start | bytes 1048576 | tf_op jit(solution)/shard_map/all_to_all | solution.py:49
  211.7 9.7 %copy-start.12 = (f32[256,1,512]{2,1,0:T(1,128)}, f32[256,1,512]{2,1,0:T(1,128)S(1)}, u32[]{:S(2)}) copy-start(f32[256,1,512]{2,1,0:T(1,128)S(1)} %all-to-all-done.9) | copy-start | bytes 1572868
  211.7 61.7 %all-to-all-start.1 = ((f32[256,1,1024]{2,1,0:T(1,128)}), f32[256,1,1024]{2,1,0:T(1,128)}, u32[]{:S(2)}, u32[]{:S(2)}) async-start(f32[256,1,1024]{2,1,0:T(1,128)} %copy.44), calls=%async_computation.1 | async-start | bytes 2097152 | tf_op jit(solution)/shard_map/all_to_all | solution.py:48
  219.3 63.0 %copy-start.11 = (f32[256,1,512]{2,1,0:T(1,128)S(1)}, f32[256,1,512]{2,1,0:T(1,128)}, u32[]{:S(2)}) copy-start(f32[256,1,512]{2,1,0:T(1,128)} %copy-done.10) | copy-start | bytes 1572868
  273.4 9.4 %copy-start.13 = (f32[256,1,512]{2,1,0:T(1,128)S(1)}, f32[256,1,512]{2,1,0:T(1,128)}, u32[]{:S(2)}) copy-start(f32[256,1,512]{2,1,0:T(1,128)} %copy-done.12) | copy-start | bytes 1572868
  273.4 63.1 %all-to-all-start.2 = ((f32[256,1,1024]{2,1,0:T(1,128)}), f32[256,1,1024]{2,1,0:T(1,128)S(1)}, u32[]{:S(2)}, u32[]{:S(2)}) async-start(f32[256,1,1024]{2,1,0:T(1,128)} %copy.46), calls=%async_computation.2 | async-start | bytes 2097152 | tf_op jit(solution)/shard_map/all_to_all | solution.py:49
  336.5 1.0 copy-start.3
  339.9 1.2 copy-start.2
  342.4 1.3 copy-start.15
  342.4 1.3 copy-start.16
  348.1 13.3 %copy-start.1 = (f32[2,128,512]{1,2,0:T(8,128)S(1)}, f32[2,128,512]{1,2,0:T(8,128)}, u32[]{:S(2)}) copy-start(f32[2,128,512]{1,2,0:T(8,128)} %get-tuple-element.8) | copy-start | bytes 1572868
  352.0 42.1 %all-to-all-start.3 = ((f32[2,128,512]{2,0,1:T(2,128)}), f32[2,128,512]{2,0,1:T(2,128)}, u32[]{:S(2)}, u32[]{:S(2)}) async-start(f32[2,128,512]{2,0,1:T(2,128)} %copy.48), calls=%async_computation.3 | async-start | bytes 1048576 | tf_op jit(solution)/shard_map/all_to_all | solution.py:76
  394.1 61.5 %all-to-all-start.10 = ((f32[2,128,1024]{2,0,1:T(2,128)}), f32[2,128,1024]{2,0,1:T(2,128)S(1)}, u32[]{:S(2)}, u32[]{:S(2)}) async-start(f32[2,128,1024]{2,0,1:T(2,128)} %copy.57), calls=%async_computation.10 | async-start | bytes 2097152 | tf_op jit(solution)/shard_map/all_to_all | solution.py:76
  401.2 62.8 %copy-start.14 = (f32[2,128,512]{1,2,0:T(8,128)S(1)}, f32[2,128,512]{1,2,0:T(8,128)}, u32[]{:S(2)}) copy-start(f32[2,128,512]{1,2,0:T(8,128)} %get-tuple-element.17) | copy-start | bytes 1572868
  455.6 62.8 %all-to-all-start.11 = ((f32[2,128,1024]{2,0,1:T(2,128)}), f32[2,128,1024]{2,0,1:T(2,128)S(1)}, u32[]{:S(2)}, u32[]{:S(2)}) async-start(f32[2,128,1024]{2,0,1:T(2,128)} %copy.58), calls=%async_computation.11 | async-start | bytes 2097152 | tf_op jit(solution)/shard_map/all_to_all | solution.py:77
  518.4 41.8 %all-to-all-start.4 = ((f32[2,128,512]{2,0,1:T(2,128)}), f32[2,128,512]{2,0,1:T(2,128)S(1)}, u32[]{:S(2)}, u32[]{:S(2)}) async-start(f32[2,128,512]{2,0,1:T(2,128)} %copy.49), calls=%async_computation.4 | async-start | bytes 1048576 | tf_op jit(solution)/shard_map/all_to_all | solution.py:77
  528.8 1.7 copy-start.4
  530.6 1.2 copy-start.5
  560.2 40.3 %all-to-all-start.12 = ((f32[128,1,1024]{2,1,0:T(1,128)}), f32[128,1,1024]{2,1,0:T(1,128)S(1)}, u32[]{:S(2)}, u32[]{:S(2)}) async-start(f32[128,1,1024]{2,1,0:T(1,128)} %copy.59), calls=%async_computation.12 | async-start | bytes 1048576 | tf_op jit(solution)/shard_map/all_to_all | solution.py:82
  569.1 61.0 %copy-start.7 = (f32[128,512]{1,0:T(8,128)S(1)}, f32[128,512]{1,0:T(8,128)}, u32[]{:S(2)}) copy-start(f32[128,512]{1,0:T(8,128)} %copy-done.6) | copy-start | bytes 786436
  569.1 61.0 %copy-start.9 = (f32[128,512]{1,0:T(8,128)S(1)}, f32[128,512]{1,0:T(8,128)}, u32[]{:S(2)}) copy-start(f32[128,512]{1,0:T(8,128)} %copy-done.8) | copy-start | bytes 786436
  569.1 61.0 %copy-start.20 = (f32[512]{0:T(512)S(1)}, f32[512]{0:T(512)}, u32[]{:S(2)}) copy-start(f32[512]{0:T(512)} %param.8) | copy-start | bytes 6148
  600.5 29.5 %all-to-all-start.5 = ((f32[128,1,512]{2,1,0:T(1,128)}), f32[128,1,512]{2,1,0:T(1,128)S(1)}, u32[]{:S(2)}, u32[]{:S(2)}) async-start(f32[128,1,512]{2,1,0:T(1,128)} %copy.50), calls=%async_computation.5 | async-start | bytes 524288 | tf_op jit(solution)/shard_map/all_to_all | solution.py:82
  631.0 16.0 %copy-start = (bf16[2048,512]{1,0:T(8,128)(2,1)S(1)}, bf16[2048,512]{1,0:T(8,128)(2,1)}, u32[]{:S(2)}) copy-start(bf16[2048,512]{1,0:T(8,128)(2,1)} %param.10) | copy-start | bytes 6291460
  631.1 17.0 %collective-permute-start.1 = (f32[3,2,512]{2,1,0:T(2,128)S(1)}, f32[3,2,512]{2,1,0:T(2,128)S(1)}, u32[]{:S(2)}, u32[]{:S(2)}) collective-permute-start(f32[3,2,512]{2,1,0:T(2,128)S(1)} %slice.85), channel_id=1, source_target_pairs={{4,0},{8,4},{12,8},{16,12},{20,16},{24,20},{28,24},{32,28},{36,32}... | collective-permute-start | bytes 36872 | tf_op jit(solution)/shard_map/ppermute | solution.py:15
where the time goes:
time: 659 us; the launch traced here: 649 us
  waiting for transfers between devices  415 us (63%)
  starting transfers between devices  125 us (19%)
  blocking collectives  36.3 us (6%)
  matrix products  35.1 us (5%)
  local copies, waits for them, and re-layouts  33.2 us (5%)
    all_to_all x2, waiting for transfers between devices, forward_spectrum(): lax.all_to_all(turned_re, 'seq', split_axis=0, concat_axis=1, tiled=True)  83.8 us
    all_to_all x2, waiting for transfers between devices, time_signal(): lax.all_to_all(turned_im, 'seq', split_axis=1, concat_axis=0, tiled=True)  79.3 us
    all_to_all x2, waiting for transfers between devices, time_signal(): lax.all_to_all(turned_re, 'seq', split_axis=1, concat_axis=0, tiled=True)  77.4 us
    all_to_all x2, waiting for transfers between devices, forward_spectrum(): lax.all_to_all(turned_im, 'seq', split_axis=0, concat_axis=1, tiled=True)  72.7 us
    all_to_all x2, waiting for transfers between devices, time_signal(): lax.all_to_all(returned, 'seq', split_axis=0, concat_axis=1, tiled=True)[0]  50.8 us
    all_to_all x2, waiting for transfers between devices, forward_spectrum(): lax.all_to_all(signal[None], 'seq', split_axis=1, concat_axis=0, tiled=True)  50.7 us
    all_to_all x2, starting transfers between devices, forward_spectrum(): lax.all_to_all(signal[None], 'seq', split_axis=1, concat_axis=0, tiled=True)  32.2 us
    dot_general x24, matrix products, contract(): jnp.einsum(pattern, matrix, values, precision=HIGHEST, preferred_element_...  32 us
  transfers between devices with their start and end apart: 15, of which 12 were waited for; matrix products, arithmetic and copies ran while one was open for 8% of the time, Pallas kernels for 0%

commit v1 on v0

v1 whole, which is shorter than its diff:
```python
import math

import jax
import jax.numpy as jnp
import numpy as np
from jax import lax
from jax.sharding import PartitionSpec as P

HIGH = lax.Precision.HIGH
BF16 = jnp.bfloat16
F32 = jnp.float32


def dft_tables(blocks, rows):
    p = np.arange(blocks)[None, :]
    c = np.arange(blocks)[:, None] + 0.5
    outer = 2 * np.pi * p * c / (2 * blocks)
    r = np.arange(rows)[None, :]
    turn = 2 * np.pi * r * c / (2 * blocks * rows)
    inner = 2 * np.pi * np.arange(rows)[:, None] * r / rows
    return [
        np.asarray(f(a), np.float32) for a in (outer, turn, inner) for f in (np.cos, np.sin)
    ]


def local(qkv, filt, skip_gain, short_weight, w_out, g_out):
    blocks = lax.axis_size("seq")
    slabs = lax.axis_size("ch")
    rows, width = qkv.shape[1:]
    own = width // blocks
    oc, os_, tc, ts, ic, is_ = dft_tables(blocks, rows)

    def passed(x, step):
        route = [(i - step, i) for i in range(blocks) if 0 <= i - step < blocks]
        return lax.ppermute(x, "seq", route)

    partial = lax.dot_general(g_out, w_out, (((1,), (1,)), ((), ())), preferred_element_type=F32)
    partial = partial.astype(BF16).reshape(rows, slabs, width)
    parts = lax.all_to_all(partial, "ch", split_axis=1, concat_axis=1, tiled=True)
    grad_gated = jnp.sum(parts.astype(F32), axis=1)

    ext = jnp.concatenate([passed(qkv[:, rows - 2 :, :], 1), qkv], axis=1).astype(F32)
    sw = short_weight[:, :, None, :]
    short = sw[:, 0] * ext[:, 2:] + sw[:, 1] * ext[:, 1:-1] + sw[:, 2] * ext[:, :-2]
    query, key, value = short[0], short[1], short[2]
    mixed = key * value
    grad_long = grad_gated * query

    def spread(signals):
        n = len(signals)
        x = jnp.stack(signals).astype(BF16).transpose(2, 0, 1).reshape(blocks, own * n, rows)
        return lax.all_to_all(x, "seq", split_axis=0, concat_axis=0, tiled=True)

    def gathered(y, n):
        x = lax.all_to_all(y, "seq", split_axis=0, concat_axis=0, tiled=True)
        return x.reshape(width, n, rows).transpose(1, 2, 0).astype(F32)

    def mm(pattern, a, b):
        return jnp.einsum(pattern, a, b, precision=HIGH, preferred_element_type=F32)

    x = spread([mixed, filt, grad_long]).astype(F32)
    outer = np.concatenate([oc, -os_], axis=0)
    s = mm("ap,pnr->nar", outer, x)
    sre, sim = s[:, :blocks], s[:, blocks:]
    tre = sre * tc + sim * ts
    tim = sim * tc - sre * ts
    w = np.block([[ic, -is_], [is_, ic]])
    spec = mm("ncr,rk->nck", jnp.concatenate([tre, tim], axis=2), w)
    spec = spec.reshape(own, 3, blocks, 2, rows)
    mre, mim = spec[:, 0, :, 0], spec[:, 0, :, 1]
    fre, fim = spec[:, 1, :, 0], spec[:, 1, :, 1]
    gre, gim = spec[:, 2, :, 0], spec[:, 2, :, 1]
    pre = jnp.stack([mre * fre - mim * fim, fre * gre + fim * gim, mre * gre + mim * gim], 1)
    pim = jnp.stack([mre * fim + mim * fre, fre * gim - fim * gre, mre * gim - mim * gre], 1)
    wi = np.block([[ic, is_], [-is_, ic]])
    z = mm("nsck,kr->nscr", jnp.concatenate([pre, pim], axis=3), wi)
    zre, zim = z[..., :rows], z[..., rows:]
    yre = zre * tc - zim * ts
    yim = zim * tc + zre * ts
    y = jnp.concatenate([yre, yim], axis=2).reshape(own * 3, 2 * blocks, rows)
    back = np.concatenate([oc.T, -os_.T], axis=1) * np.float32(1.0 / (blocks * rows))
    t = mm("pa,nar->pnr", back, y).astype(BF16)
    conv, corr, gfil = gathered(t, 3)

    long_out = conv + skip_gain * mixed
    gated = (query * long_out).astype(BF16)
    sent = jnp.broadcast_to(gated[:, None], (rows, slabs, width))
    every = lax.all_to_all(sent, "ch", split_axis=1, concat_axis=1, tiled=True)
    output = jnp.dot(
        every.reshape(rows, slabs * width), w_out, preferred_element_type=F32
    ).astype(BF16)
    grad_query = grad_gated * long_out
    grad_mixed = corr + skip_gain * grad_long
    grad_filter = gfil * (1.0 / math.sqrt(blocks * rows))
    gs = jnp.stack([grad_query, grad_mixed * value, grad_mixed * key])
    extg = jnp.concatenate([gs, passed(gs[:, :2, :], -1)], axis=1)
    grad_qkv = sw[:, 0] * extg[:, :-2] + sw[:, 1] * extg[:, 1:-1] + sw[:, 2] * extg[:, 2:]
    return (output, grad_qkv.astype(BF16), grad_filter)


def solution(mesh):
    in_specs = (
        P(None, "seq", "ch"),
        P("seq", "ch"),
        P("ch"),
        P(None, None, "ch"),
        P(None, "ch"),
        P("seq", "ch"),
    )
    out_specs = (P("seq", "ch"), P(None, "seq", "ch"), P("seq", "ch"))
    return jax.shard_map(local, mesh=mesh, in_specs=in_specs, out_specs=out_specs, check_vma=False)
```

time: 659 us -> 163 us (0.25); the launches traced: 649 us -> 162 us
  waiting for transfers between devices: 415 us -> 13.1 us
  starting transfers between devices: 125 us -> 15.6 us
  blocking collectives: 36.3 us -> 95.5 us
  matrix products: 35.1 us -> 8.31 us
  local copies, waits for them, and re-layouts: 33.2 us -> 20.5 us
    all_to_all x13 -> x2, waiting for transfers between devices: 415 us -> 13.1 us  [the longest x1 7.62 us: local(): every = lax.all_to_all(sent, 'ch', split_axis=1, concat_axis=1, tiled=True)]
    all_to_all x13 -> x2, starting transfers between devices: 116 us -> 7.61 us  [the longest x1 4.01 us: local(): lax.all_to_all(partial, 'ch', split_axis=1, concat_axis=1, tiled=True)]
    all_to_all x0 -> x2, blocking collectives: none -> 95.5 us  [the longest x1 55 us: spread(): return lax.all_to_all(x, 'seq', split_axis=0, concat_axis=0, tiled=True)]
    all_gather x2 -> x0, blocking collectives: 36.3 us -> none  [the longest x1 24.7 us: local(): grad_all = lax.all_gather(g_out, 'ch', axis=1, tiled=True)]
    dot_general x26 -> x6, matrix products: 35.1 us -> 8.31 us  [the longest x4 5.46 us: mm(): return jnp.einsum(pattern, a, b, precision=HIGH, preferred_element_type=F32)]
    sub x4 -> x0, local copies, waits for them, and re-layouts: 7.74 us -> none  [the longest x2 4.29 us: time_signal(): turned_re = back_re * twist_cos - back_im * twist_sin]
    all_to_all x5 -> x1, local copies, waits for them, and re-layouts: 7.83 us -> 0.27 us  [local(): every = lax.all_to_all(sent, 'ch', split_axis=1, concat_axis=1, tiled=True)]
  transfers between devices with their start and end apart: 15 -> 4, of which waited for: 12 -> 2; matrix products, arithmetic and copies ran while one was open for 8% -> 5% of each run, Pallas kernels for 0% -> 0%
where the time goes in v1:
time: 163 us; the launch traced here: 162 us
  blocking collectives  95.5 us (59%)
  local copies, waits for them, and re-layouts  20.5 us (13%)
  starting transfers between devices  15.6 us (10%)
  waiting for transfers between devices  13.1 us (8%)
  other arithmetic  8.33 us (5%)
  matrix products  8.31 us (5%)
    all_to_all x1, blocking collectives, spread(): return lax.all_to_all(x, 'seq', split_axis=0, concat_axis=0, tiled=True)  55 us
    all_to_all x1, blocking collectives, gathered(): x = lax.all_to_all(y, 'seq', split_axis=0, concat_axis=0, tiled=True)  40.5 us
    ppermute x2, starting transfers between devices, passed(): return lax.ppermute(x, 'seq', route)  8.01 us
    all_to_all x1, waiting for transfers between devices, local(): every = lax.all_to_all(sent, 'ch', split_axis=1, concat_axis=1, tiled=True)  7.62 us
    dot_general x4, matrix products, mm(): return jnp.einsum(pattern, a, b, precision=HIGH, preferred_element_type=F32)  5.46 us
    all_to_all x1, waiting for transfers between devices, local(): lax.all_to_all(partial, 'ch', split_axis=1, concat_axis=1, tiled=True)  5.45 us
    all_to_all x1, starting transfers between devices, local(): lax.all_to_all(partial, 'ch', split_axis=1, concat_axis=1, tiled=True)  4.01 us
    convert_element_type x2, local copies, waits for them, and re-layouts, gathered(): return x.reshape(width, n, rows).transpose(1, 2, 0).astype(F32)  3.79 us
  transfers between devices with their start and end apart: 4, of which 2 were waited for; matrix products, arithmetic and copies ran while one was open for 5% of the time, Pallas kernels for 0%

profile of v1, /device:TPU:1, one launch (start us, length us, event | category | flops | bytes accessed | tf_op | source)
XLA Modules:
  0.0 162.3 jit_solution(2980552042398264160)
XLA Ops:
  0.6 0.0 copy-start
  0.6 1.5 slice.73
  2.1 4.9 %collective-permute-start = (bf16[3,2,512]{2,1,0:T(2,128)(2,1)}, bf16[3,2,512]{2,1,0:T(2,128)(2,1)}, u32[]{:S(2)}, u32[]{:S(2)}) collective-permute-start(bf16[3,2,512]{2,1,0:T(2,128)(2,1)} %slice.73), channel_id=1, source_target_pairs={{0,4},{4,8},{8,12},{12,16},{16,20},{20,24},{24,28},{28,32},{32,36}... | collective-permute-start | bytes 18440 | tf_op jit(solution)/shard_map/ppermute | solution.py:35
  7.1 1.7 %convolution_convert_fusion = bf16[128,2048]{1,0:T(8,128)(2,1)S(1)} fusion(bf16[128,512]{1,0:T(8,128)(2,1)} %param.17, bf16[2048,512]{1,0:T(8,128)(2,1)S(1)} %copy-done), kind=kOutput, calls=%fused_computation | convolution fusion | flops 268697600 | bytes 2752512 | tf_op jit(solution)/shard_map/dot_general | solution.py:37
  8.8 0.9 copy.130
  9.7 4.0 %all-to-all-start = ((bf16[128,4,512]{2,0,1:T(8,128)(2,1)}), bf16[128,4,512]{2,0,1:T(8,128)(2,1)S(1)}, u32[]{:S(2)}, u32[]{:S(2)}) async-start(bf16[128,4,512]{2,0,1:T(8,128)(2,1)} %bitcast.80), calls=%async_computation | async-start | bytes 1048576 | tf_op jit(solution)/shard_map/all_to_all | solution.py:39
  13.8 1.1 maximum_convert_fusion
  14.9 0.2 fusion.16
  15.2 5.4 %all-to-all-done = bf16[128,4,512]{2,0,1:T(8,128)(2,1)S(1)} async-done(((bf16[128,4,512]{2,0,1:T(8,128)(2,1)}), bf16[128,4,512]{2,0,1:T(8,128)(2,1)S(1)}, u32[]{:S(2)}, u32[]{:S(2)}) %all-to-all-start) | async-done | bytes 524320 | tf_op jit(solution)/shard_map/all_to_all | solution.py:39
  20.6 0.1 convert_reduce_fusion
  20.7 0.7 copy-done.3
  21.4 0.1 fusion.26
  21.5 0.8 maximum_bitcast_fusion
  22.3 1.3 copy.90
  23.6 1.1 reshape.326
  24.8 55.0 %all_to_all.20 = bf16[128,12,128]{2,1,0:T(8,128)(2,1)S(1)} all-to-all(bf16[128,12,128]{2,1,0:T(8,128)(2,1)} %reshape.326), channel_id=1, replica_groups=mesh['seq'=128,'ch'=4] {'seq'}, dimensions={0} | all-to-all | bytes 786432 | tf_op jit(solution)/shard_map/all_to_all | solution.py:52
  79.8 0.6 convolution_bitcast_fusion
  80.4 0.0 copy-start.5
  80.4 0.2 multiply_add_fusion.1
  80.6 0.7 copy-done.5
  81.4 2.6 %fusion = f32[12,128,256]{2,1,0:T(8,128)} fusion(f32[256,256,1]{1,0,2:T(8,128)S(1)} %copy-done.5, f32[12,128,128]{1,2,0:T(8,128)S(1)} %get-tuple-element.12, f32[12,128,128]{1,2,0:T(8,128)S(1)} %get-tuple-element.11), kind=kOutput, calls=%fused_computation.1 | convolution fusion | flops 604372992 | bytes 3407872 | tf_op jit(solution)/shard_map/ncr,rk->nck/dot_general | solution.py:59
  84.0 2.9 %reshape.327 = f32[4,3,128,2,128]{4,3,2,1,0:T(2,128)} reshape(f32[12,128,256]{2,1,0:T(8,128)} %fusion) | data formatting | bytes 3145728 | tf_op jit(solution)/shard_map/reshape | solution.py:69
  86.9 3.5 %fusion.27 = (f32[4,1,128,1,128]{4,3,2,1,0:T(1,128)S(1)}, f32[4,1,128,1,128]{4,3,2,1,0:T(1,128)S(1)}, f32[4,1,128,1,128]{4,3,2,1,0:T(1,128)S(1)}, f32[4,1,128,1,...) fusion(f32[4,3,128,2,128]{4,3,2,1,0:T(2,128)} %reshape.327), kind=kLoop, calls=%fused_computation.66 | loop fusion | bytes 3145728 | tf_op jit(solution)/shard_map/slice | solution.py:71
  90.4 0.0 copy-start.16
  90.4 0.2 subtract_bitcast_fusion.2
  90.7 0.7 copy-done.16
  91.4 0.8 fusion.4
  92.2 0.0 copy-done.10
  92.2 0.0 copy-done.11
  92.2 0.2 multiply_subtract_fusion
  92.5 0.1 pad_maximum_fusion
  92.6 0.8 copy-done.6
  93.4 1.4 fusion.12
  94.8 1.2 copy.105
  96.0 40.5 %all_to_all.21 = bf16[128,12,128]{2,1,0:T(8,128)(2,1)S(1)} all-to-all(bf16[128,12,128]{2,1,0:T(8,128)(2,1)} %copy.105), channel_id=1, replica_groups=mesh['seq'=128,'ch'=4] {'seq'}, dimensions={0} | all-to-all | bytes 786432 | tf_op jit(solution)/shard_map/all_to_all | solution.py:55
  136.5 1.4 reshape.330
  137.9 2.4 %copy.106 = f32[512,3,128]{0,2,1:T(8,128)} copy(f32[512,3,128]{2,1,0:T(4,128)} %reshape.330) | data formatting | bytes 1572864 | tf_op jit(solution)/shard_map/convert_element_type | solution.py:56
  140.3 2.1 %slice_multiply_fusion.6 = (f32[1,128,512]{2,1,0:T(8,128)S(1)}, f32[1,128,512]{2,1,0:T(8,128)S(1)}, f32[1,128,512]{2,1,0:T(8,128)S(1)}, f32[128,512]{1,0:T(8,128)}) fusion(f32[3,128,512]{2,1,0:T(8,128)S(1)} %fusion.16, f32[128,512]{1,0:T(8,128)} %copy-done.3, f32[512]{0:T(512)S(1)} %copy-done.15, f32[3,128,512]{2,1,0:T(8,128)} %bitcast.83), kind=kLoop, calls=%fused_computation.55 | loop fusion | flops 589824 | bytes 2885632 | tf_op jit(solution)/shard_map/mul | solution.py:95
  142.5 0.1 pad_maximum_fusion.3
  142.6 3.1 %collective-permute-start.1 = (f32[3,2,512]{2,1,0:T(2,128)S(1)}, f32[3,2,512]{2,1,0:T(2,128)S(1)}, u32[]{:S(2)}, u32[]{:S(2)}) collective-permute-start(f32[3,2,512]{2,1,0:T(2,128)S(1)} %slice.114), channel_id=1, source_target_pairs={{4,0},{8,4},{12,8},{16,12},{20,16},{24,20},{28,24},{32,28},{36,32}... | collective-permute-start | bytes 36872 | tf_op jit(solution)/shard_map/ppermute | solution.py:35
  145.7 1.0 fusion.22
  146.7 0.9 broadcast_in_dim.5
  147.6 3.6 %all-to-all-start.3 = ((bf16[128,4,512]{2,0,1:T(8,128)(2,1)}), bf16[128,4,512]{2,0,1:T(8,128)(2,1)S(1)}, u32[]{:S(2)}, u32[]{:S(2)}) async-start(bf16[128,4,512]{2,0,1:T(8,128)(2,1)} %broadcast_in_dim.5), calls=%async_computation.3 | async-start | bytes 1048576 | tf_op jit(solution)/shard_map/all_to_all | solution.py:88
  151.2 1.0 pad_maximum_fusion.1
  152.2 1.0 fusion.14
  153.2 7.6 %all-to-all-done.3 = bf16[128,4,512]{2,0,1:T(8,128)(2,1)S(1)} async-done(((bf16[128,4,512]{2,0,1:T(8,128)(2,1)}), bf16[128,4,512]{2,0,1:T(8,128)(2,1)S(1)}, u32[]{:S(2)}, u32[]{:S(2)}) %all-to-all-start.3) | async-done | bytes 524320 | tf_op jit(solution)/shard_map/all_to_all | solution.py:88
  160.9 0.3 copy.107
  161.1 1.1 convolution_convert_fusion.2
  (33 shorter events, 0.2 us)
Async XLA Ops:
  0.6 6.4 %copy-start = (bf16[2048,512]{1,0:T(8,128)(2,1)S(1)}, bf16[2048,512]{1,0:T(8,128)(2,1)}, u32[]{:S(2)}) copy-start(bf16[2048,512]{1,0:T(8,128)(2,1)} %param.16) | copy-start | bytes 6291460
  2.1 11.6 %collective-permute-start = (bf16[3,2,512]{2,1,0:T(2,128)(2,1)}, bf16[3,2,512]{2,1,0:T(2,128)(2,1)}, u32[]{:S(2)}, u32[]{:S(2)}) collective-permute-start(bf16[3,2,512]{2,1,0:T(2,128)(2,1)} %slice.73), channel_id=1, source_target_pairs={{0,4},{4,8},{8,12},{12,16},{16,20},{20,24},{24,28},{28,32},{32,36}... | collective-permute-start | bytes 18440 | tf_op jit(solution)/shard_map/ppermute | solution.py:35
  8.8 4.9 %copy-start.14 = (f32[3,3,512]{2,1,0:T(4,128)S(1)}, f32[3,3,512]{2,1,0:T(4,128)}, u32[]{:S(2)}) copy-start(f32[3,3,512]{2,1,0:T(4,128)} %param.15) | copy-start | bytes 55300
  8.8 4.9 %copy-start.4 = (f32[128,512]{1,0:T(8,128)S(1)}, f32[128,512]{1,0:T(8,128)}, u32[]{:S(2)}) copy-start(f32[128,512]{1,0:T(8,128)} %param.13) | copy-start | bytes 786436
  9.7 10.9 %all-to-all-start = ((bf16[128,4,512]{2,0,1:T(8,128)(2,1)}), bf16[128,4,512]{2,0,1:T(8,128)(2,1)S(1)}, u32[]{:S(2)}, u32[]{:S(2)}) async-start(bf16[128,4,512]{2,0,1:T(8,128)(2,1)} %bitcast.80), calls=%async_computation | async-start | bytes 1048576 | tf_op jit(solution)/shard_map/all_to_all | solution.py:39
  13.8 1.2 copy-start.8
  20.7 0.7 copy-start.3
  22.3 57.5 %copy-start.7 = (f32[256,128,1]{1,0,2:T(8,128)S(1)}, f32[256,128,1]{1,0,2:T(8,128)}, u32[]{:S(2)}) copy-start(f32[256,128,1]{1,0,2:T(8,128)} %constant.22) | copy-start | bytes 393220
  24.8 55.6 %copy-start.12 = (f32[128,128]{0,1:T(8,128)S(1)}, f32[128,128]{0,1:T(8,128)}, u32[]{:S(2)}) copy-start(f32[128,128]{0,1:T(8,128)} %constant.18.clone) | copy-start | bytes 196612
  24.8 55.6 %copy-start.13 = (f32[128,128]{0,1:T(8,128)S(1)}, f32[128,128]{0,1:T(8,128)}, u32[]{:S(2)}) copy-start(f32[128,128]{0,1:T(8,128)} %constant.17.clone) | copy-start | bytes 196612
  80.4 1.0 copy-start.5
  90.4 1.0 copy-start.16
  91.4 0.8 copy-start.10
  91.4 0.9 copy-start.11
  92.5 0.9 copy-start.6
  136.5 3.8 %copy-start.15 = (f32[512]{0:T(512)S(1)}, f32[512]{0:T(512)}, u32[]{:S(2)}) copy-start(f32[512]{0:T(512)} %param.14) | copy-start | bytes 6148
  142.5 4.2 %copy-start.1 = (f32[1,128,512]{2,1,0:T(8,128)}, f32[1,128,512]{2,1,0:T(8,128)S(1)}, u32[]{:S(2)}) copy-start(f32[1,128,512]{2,1,0:T(8,128)S(1)} %slice_multiply_fusion.8) | copy-start | bytes 786436
  142.6 8.6 %collective-permute-start.1 = (f32[3,2,512]{2,1,0:T(2,128)S(1)}, f32[3,2,512]{2,1,0:T(2,128)S(1)}, u32[]{:S(2)}, u32[]{:S(2)}) collective-permute-start(f32[3,2,512]{2,1,0:T(2,128)S(1)} %slice.114), channel_id=1, source_target_pairs={{4,0},{8,4},{12,8},{16,12},{20,16},{24,20},{28,24},{32,28},{36,32}... | collective-permute-start | bytes 36872 | tf_op jit(solution)/shard_map/ppermute | solution.py:35
  146.7 5.5 %copy-start.9 = (f32[3,1,1,512]{3,0,1,2:T(4,128)S(1)}, f32[3,1,1,512]{3,0,1,2:T(4,128)}, u32[]{:S(2)}) copy-start(f32[3,1,1,512]{3,0,1,2:T(4,128)} %copy-done.8) | copy-start | bytes 18436
  147.6 4.7 %copy-start.2 = (f32[1,128,512]{2,1,0:T(8,128)S(1)}, f32[1,128,512]{2,1,0:T(8,128)}, u32[]{:S(2)}) copy-start(f32[1,128,512]{2,1,0:T(8,128)} %copy-done.1) | copy-start | bytes 786436
  147.6 13.3 %all-to-all-start.3 = ((bf16[128,4,512]{2,0,1:T(8,128)(2,1)}), bf16[128,4,512]{2,0,1:T(8,128)(2,1)S(1)}, u32[]{:S(2)}, u32[]{:S(2)}) async-start(bf16[128,4,512]{2,0,1:T(8,128)(2,1)} %broadcast_in_dim.5), calls=%async_computation.3 | async-start | bytes 1048576 | tf_op jit(solution)/shard_map/all_to_all | solution.py:88

commit v2 on v1

v2 whole, which is shorter than its diff:
```python
import functools
import math

import jax
import jax.numpy as jnp
import numpy as np
from jax import lax
from jax.experimental import pallas as pl
from jax.experimental.pallas import tpu as pltpu
from jax.sharding import PartitionSpec as P

BF16 = jnp.bfloat16
F32 = jnp.float32
MESH = pl.DeviceIdType.MESH
Z_CHIPS = 16
OWN = 4
FILT, MIXED, GRAD, CONV, CORR, GFIL = range(6)


def split_const(a):
    high = a.astype(BF16)
    return high, (a - high.astype(np.float64)).astype(BF16)


def dft_tables(blocks, rows, z_chips):
    q = np.arange(blocks)
    yc, z = q // z_chips, q % z_chips
    p = ((yc // 2) * z_chips + z) * 2 + yc % 2
    c = np.arange(blocks)[:, None] + 0.5
    outer = 2 * np.pi * p[None, :] * c / (2 * blocks)
    r = np.arange(rows)[None, :]
    turn = 2 * np.pi * r * c / (2 * blocks * rows)
    inner = 2 * np.pi * np.arange(rows)[:, None] * r / rows
    ahead = np.concatenate([np.cos(outer), -np.sin(outer)], axis=0)
    ic, is_ = np.cos(inner), np.sin(inner)
    mix = np.block([[ic, -is_], [is_, ic]])
    unmix = np.block([[ic, is_], [-is_, ic]])
    return (
        *split_const(ahead),
        *split_const(ahead.T / (blocks * rows)),
        *split_const(mix),
        *split_const(unmix),
        np.cos(turn).astype(np.float32),
        np.sin(turn).astype(np.float32),
    )


def dot(a, b):
    return jnp.dot(a, b, preferred_element_type=F32)


def halves(a):
    high = a.astype(BF16)
    return high, (a - high.astype(F32)).astype(BF16)


def kernel(
    shape,
    qkv, filt, skip, sw, w_out, g_out,
    ah, al, bh, bl, mh, ml, uh, ul, tcos, tsin,
    output, grad_qkv, grad_filter,
    send, mid, recv, halo, ghalo_out, ghalo_in, part_out, part_in, gate_out, gate_in,
    xs, ext, spec, gs, shorts, gg, glong,
    send1, recv1, send2, recv2, loc1, loc2, hsem, psend, precv, gsend, grecv,
):
    blocks, zn, slabs, rows, width = shape
    lines = blocks // zn
    s = lax.axis_index("seq")
    ch = lax.axis_index("ch")
    core = s % 2
    z = (s // 2) % zn
    y = s // (2 * zn)
    yc = y * 2 + core

    def on_z(i):
        dz = zn // 2 + ((i + 1) // 2) * (1 - 2 * (i % 2))
        other = (z + dz) % zn
        return other, (y * zn + other) * 2 + core

    def on_line(i):
        other = (yc + 1 + i) % lines
        return other, ((other // 2) * zn + z) * 2 + other % 2

    after = (s + 1) % blocks
    before = (s + blocks - 1) % blocks

    barrier = pltpu.get_barrier_semaphore()

    def greet(a, b):
        pl.semaphore_signal(barrier, inc=1, device_id=(a, b), device_id_type=MESH)

    def greet_z(i, _):
        greet(on_z(i)[1], ch)
        return 0

    def greet_line(i, _):
        greet(on_line(i)[1], ch)
        return 0

    lax.fori_loop(0, zn - 1, greet_z, 0)
    lax.fori_loop(0, lines - 1, greet_line, 0)
    for i in range(1, slabs):
        greet(s, (ch + i) % slabs)
    greet(after, ch)
    greet(before, ch)

    def slab(k):
        return w_out[pl.ds(pl.multiple_of(k * width, width), width), :]

    def rows_of(k):
        return lax.dot_general(
            g_out[...], slab(k), (((1,), (1,)), ((), ())), preferred_element_type=F32
        )

    def pack(u, value):
        send[u] = jnp.swapaxes(value, 0, 1).astype(BF16).reshape(lines, zn, OWN, rows)

    def unpack(u):
        return jnp.swapaxes(recv[u].astype(F32).reshape(width, rows), 0, 1)

    def own1(u):
        return pltpu.make_async_copy(send.at[u, :, z], mid.at[u, z], loc1.at[u])

    def own2(u):
        return pltpu.make_async_copy(mid.at[u, :, yc], recv.at[u, yc], loc2.at[u])

    def start1(u):
        def go(i, _):
            other, device = on_z(i)
            pltpu.make_async_remote_copy(
                src_ref=send.at[u, :, other],
                dst_ref=mid.at[u, z],
                send_sem=send1.at[u],
                recv_sem=recv1.at[u],
                device_id=(device, ch),
                device_id_type=MESH,
            ).start()
            return 0

        lax.fori_loop(0, zn - 1, go, 0)
        own1(u).start()

    def start2(u):
        own1(u).wait()
        landed = mid.at[u, pl.ds(0, zn - 1)]
        pltpu.make_async_copy(landed, landed, recv1.at[u]).wait()

        def go(i, _):
            other, device = on_line(i)
            pltpu.make_async_remote_copy(
                src_ref=mid.at[u, :, other],
                dst_ref=recv.at[u, yc],
                send_sem=send2.at[u],
                recv_sem=recv2.at[u],
                device_id=(device, ch),
                device_id_type=MESH,
            ).start()
            return 0

        lax.fori_loop(0, lines - 1, go, 0)
        own2(u).start()

    def finish(u):
        own2(u).wait()
        landed = recv.at[u, pl.ds(0, lines - 1)]
        pltpu.make_async_copy(landed, landed, recv2.at[u]).wait()

    def drain(u):
        sent = mid.at[u, pl.ds(0, zn - 1)]
        pltpu.make_async_copy(sent, sent, send1.at[u]).wait()
        sent = recv.at[u, pl.ds(0, lines - 1)]
        pltpu.make_async_copy(sent, sent, send2.at[u]).wait()

    def to_slab(i, k, src, dst, ssem, rsem):
        return pltpu.make_async_remote_copy(
            src_ref=src,
            dst_ref=dst,
            send_sem=ssem.at[i],
            recv_sem=rsem.at[i],
            device_id=(s, k),
            device_id_type=MESH,
        )

    halo_copy = pltpu.make_async_remote_copy(
        src_ref=qkv.at[:, pl.ds(rows - 8, 8), :],
        dst_ref=halo,
        send_sem=hsem.at[0],
        recv_sem=hsem.at[1],
        device_id=(after, ch),
        device_id_type=MESH,
    )
    ghalo_copy = pltpu.make_async_remote_copy(
        src_ref=ghalo_out,
        dst_ref=ghalo_in,
        send_sem=hsem.at[2],
        recv_sem=hsem.at[3],
        device_id=(before, ch),
        device_id_type=MESH,
    )
    part_copies = [
        to_slab(i, (ch + i + 1) % slabs, part_out.at[i], part_in.at[i], psend, precv)
        for i in range(slabs - 1)
    ]
    gate_copies = [
        to_slab(i, (ch + i + 1) % slabs, gate_out, gate_in.at[i], gsend, grecv)
        for i in range(slabs - 1)
    ]

    def ahead(u, k):
        xs[...] = recv[u].astype(F32).reshape(width, rows)
        x = jnp.concatenate(
            [xs[pl.ds(j, blocks, stride=OWN), :] for j in range(OWN)], axis=1
        ).astype(BF16)
        t = dot(ah[...], x) + dot(al[...], x)
        tc, ts = tcos[...], tsin[...]
        turned = []
        for j in range(OWN):
            re = t[:blocks, j * rows : (j + 1) * rows]
            im = t[blocks:, j * rows : (j + 1) * rows]
            turned.append(jnp.concatenate([re * tc + im * ts, im * tc - re * ts], axis=1))
        high, low = halves(jnp.concatenate(turned, axis=0))
        spec[k] = dot(high, mh[...]) + dot(low, mh[...]) + dot(high, ml[...])

    def back(u, re, im):
        high, low = halves(jnp.concatenate([re, im], axis=1))
        t = dot(high, uh[...]) + dot(low, uh[...]) + dot(high, ul[...])
        tc, ts = tcos[...], tsin[...]
        turned = []
        for j in range(OWN):
            re = t[j * blocks : (j + 1) * blocks, :rows]
            im = t[j * blocks : (j + 1) * blocks, rows:]
            turned.append(jnp.concatenate([re * tc - im * ts, im * tc + re * ts], axis=0))
        high, low = halves(jnp.concatenate(turned, axis=1))
        t = dot(bh[...], high) + dot(bl[...], high) + dot(bh[...], low)
        for j in range(OWN):
            xs[pl.ds(j, blocks, stride=OWN), :] = t[:, j * rows : (j + 1) * rows]
        send[u] = xs[...].astype(BF16).reshape(lines, zn, OWN, rows)

    for i in range(slabs - 1):
        part_out[i] = rows_of((ch + i + 1) % slabs).astype(BF16)
    pack(FILT, filt[...])
    gg[...] = rows_of(ch)
    pl.semaphore_wait(barrier, zn - 1 + lines - 1 + slabs - 1 + 2)

    halo_copy.start()
    for copy in part_copies:
        copy.start()
    start1(FILT)

    halo_copy.wait_recv()
    for i in range(3):
        head = halo[i].astype(F32)
        ext[pl.ds(0, 8), :] = jnp.where(s > 0, head, jnp.zeros_like(head))
        ext[pl.ds(8, rows), :] = qkv[i].astype(F32)
        shorts[i] = (
            sw[i, pl.ds(0, 1), :] * ext[pl.ds(8, rows), :]
            + sw[i, pl.ds(1, 1), :] * ext[pl.ds(7, rows), :]
            + sw[i, pl.ds(2, 1), :] * ext[pl.ds(6, rows), :]
        )
    pack(MIXED, shorts[1] * shorts[2])
    start1(MIXED)

    total = gg[...]
    for i in range(slabs - 1):
        part_copies[i].wait_recv()
        total = total + part_in[i].astype(F32)
    gg[...] = total
    glong[...] = total * shorts[0]
    pack(GRAD, glong[...])
    start1(GRAD)

    start2(FILT)
    start2(MIXED)
    finish(FILT)
    ahead(FILT, 0)
    finish(MIXED)
    ahead(MIXED, 1)

    fre, fim = spec[0, :, :rows], spec[0, :, rows:]
    mre, mim = spec[1, :, :rows], spec[1, :, rows:]
    back(CONV, mre * fre - mim * fim, mre * fim + mim * fre)
    start1(CONV)
    start2(GRAD)
    finish(GRAD)
    ahead(GRAD, 2)
    fre, fim = spec[0, :, :rows], spec[0, :, rows:]
    gre, gim = spec[2, :, :rows], spec[2, :, rows:]
    back(CORR, fre * gre + fim * gim, fre * gim - fim * gre)
    start1(CORR)
    start2(CONV)
    mre, mim = spec[1, :, :rows], spec[1, :, rows:]
    gre, gim = spec[2, :, :rows], spec[2, :, rows:]
    back(GFIL, mre * gre + mim * gim, mre * gim - mim * gre)
    start1(GFIL)

    finish(CONV)
    long_out = unpack(CONV) + skip[...] * (shorts[1] * shorts[2])
    gate_out[...] = (shorts[0] * long_out).astype(BF16)
    for copy in gate_copies:
        copy.start()
    gs[0] = gg[...] * long_out

    start2(CORR)
    total = dot(gate_out[...], slab(ch))
    for i in range(slabs - 1):
        gate_copies[i].wait_recv()
        total = total + dot(gate_in[i], slab((ch + slabs - 1 - i) % slabs))
    output[...] = total.astype(BF16)

    start2(GFIL)
    finish(CORR)
    grad_mixed = unpack(CORR) + skip[...] * glong[...]
    gs[1] = grad_mixed * shorts[2]
    gs[2] = grad_mixed * shorts[1]
    ghalo_out[...] = gs[:, pl.ds(0, 8), :]
    ghalo_copy.start()

    finish(GFIL)
    grad_filter[...] = unpack(GFIL) * (1.0 / math.sqrt(blocks * rows))

    ghalo_copy.wait_recv()
    for i in range(3):
        tail = ghalo_in[i]
        ext[pl.ds(0, rows), :] = gs[i]
        ext[pl.ds(rows, 8), :] = jnp.where(s < blocks - 1, tail, jnp.zeros_like(tail))
        grad_qkv[i] = (
            sw[i, pl.ds(0, 1), :] * ext[pl.ds(0, rows), :]
            + sw[i, pl.ds(1, 1), :] * ext[pl.ds(1, rows), :]
            + sw[i, pl.ds(2, 1), :] * ext[pl.ds(2, rows), :]
        ).astype(BF16)

    halo_copy.wait_send()
    ghalo_copy.wait_send()
    for copy in part_copies + gate_copies:
        copy.wait_send()
    for u in range(6):
        drain(u)


def local(qkv, filt, skip_gain, short_weight, w_out, g_out):
    blocks = lax.axis_size("seq")
    slabs = lax.axis_size("ch")
    rows, width = qkv.shape[1:]
    zn = Z_CHIPS
    lines = blocks // zn
    tables = dft_tables(blocks, rows, zn)
    vmem = pl.BlockSpec(memory_space=pltpu.VMEM)
    unit = (6, lines, zn, OWN, rows)
    dma = pltpu.SemaphoreType.DMA
    return pl.pallas_call(
        functools.partial(kernel, (blocks, zn, slabs, rows, width)),
        out_shape=(
            jax.ShapeDtypeStruct((rows, width), BF16),
            jax.ShapeDtypeStruct((3, rows, width), BF16),
            jax.ShapeDtypeStruct((rows, width), F32),
        ),
        in_specs=[vmem] * (6 + len(tables)),
        out_specs=(vmem, vmem, vmem),
        scratch_shapes=[
            pltpu.VMEM(unit, BF16),
            pltpu.VMEM((6, zn, lines, OWN, rows), BF16),
            pltpu.VMEM(unit, BF16),
            pltpu.VMEM((3, 8, width), BF16),
            pltpu.VMEM((3, 8, width), F32),
            pltpu.VMEM((3, 8, width), F32),
            pltpu.VMEM((slabs - 1, rows, width), BF16),
            pltpu.VMEM((slabs - 1, rows, width), BF16),
            pltpu.VMEM((rows, width), BF16),
            pltpu.VMEM((slabs - 1, rows, width), BF16),
            pltpu.VMEM((width, rows), F32),
            pltpu.VMEM((rows + 8, width), F32),
            pltpu.VMEM((3, OWN * blocks, 2 * rows), F32),
            pltpu.VMEM((3, rows, width), F32),
            pltpu.VMEM((3, rows, width), F32),
            pltpu.VMEM((rows, width), F32),
            pltpu.VMEM((rows, width), F32),
            dma((6,)), dma((6,)), dma((6,)), dma((6,)), dma((6,)), dma((6,)),
            dma((4,)),
            dma((slabs - 1,)), dma((slabs - 1,)), dma((slabs - 1,)), dma((slabs - 1,)),
        ],
        compiler_params=pltpu.CompilerParams(collective_id=0, has_side_effects=True),
    )(qkv, filt, skip_gain[None, :], short_weight, w_out, g_out, *tables)


def solution(mesh):
    in_specs = (
        P(None, "seq", "ch"),
        P("seq", "ch"),
        P("ch"),
        P(None, None, "ch"),
        P(None, "ch"),
        P("seq", "ch"),
    )
    out_specs = (P("seq", "ch"), P(None, "seq", "ch"), P("seq", "ch"))
    return jax.shard_map(local, mesh=mesh, in_specs=in_specs, out_specs=out_specs, check_vma=False)
```

time: 163 us -> 75.3 us (0.46)
  blocking collectives: 95.5 us -> 0 us
  Pallas kernels: 0 us -> 69.4 us
  starting transfers between devices: 15.6 us -> 0 us
  local copies, waits for them, and re-layouts: 20.5 us -> 5 us
  waiting for transfers between devices: 13.1 us -> 0 us
  other arithmetic: 8.33 us -> 0 us
  matrix products: 8.31 us -> 0 us
    all_to_all x2 -> x0, blocking collectives: 95.5 us -> none  [the longest x1 55 us: spread(): return lax.all_to_all(x, 'seq', split_axis=0, concat_axis=0, tiled=True)]
    pallas_call x0 -> x1, Pallas kernels: none -> 69.4 us  [local(): pl.pallas_call(functools.partial(kernel, (blocks, zn, slabs, rows, width)...]
    all_to_all x2 -> x0, waiting for transfers between devices: 13.1 us -> none  [the longest x1 7.62 us: local(): every = lax.all_to_all(sent, 'ch', split_axis=1, concat_axis=1, tiled=True)]
    dot_general x6 -> x0, matrix products: 8.31 us -> none  [the longest x4 5.46 us: mm(): return jnp.einsum(pattern, a, b, precision=HIGH, preferred_element_type=F32)]
    ppermute x2 -> x0, starting transfers between devices: 8.01 us -> none  [passed(): return lax.ppermute(x, 'seq', route)]
    all_to_all x2 -> x0, starting transfers between devices: 7.61 us -> none  [the longest x1 4.01 us: local(): lax.all_to_all(partial, 'ch', split_axis=1, concat_axis=1, tiled=True)]
    slice x4 -> x0, local copies, waits for them, and re-layouts: 5.04 us -> none  [the longest x1 3.53 us: local(): fre, fim = (spec[:, 1, :, 0], spec[:, 1, :, 1])]
    convert_element_type x3 -> x0, local copies, waits for them, and re-layouts: 5 us -> none  [the longest x2 3.79 us: gathered(): return x.reshape(width, n, rows).transpose(1, 2, 0).astype(F32)]
  transfers between devices with their start and end apart: 4 -> 0, of which waited for: 2 -> 0; matrix products, arithmetic and copies ran while one was open for 5% -> 0% of each run, Pallas kernels for 0% -> 0%
where the time goes in v2:
time: 75.3 us; the launch traced here: 75.1 us
  Pallas kernels  69.4 us (92%)
  local copies, waits for them, and re-layouts  5 us (7%)
    pallas_call x1, Pallas kernels, local(): pl.pallas_call(functools.partial(kernel, (blocks, zn, slabs, rows, width)...  69.4 us
    unnamed x3, local copies, waits for them, and re-layouts  5 us

profile of v2, /device:TPU:1, one launch (start us, length us, event | category | flops | bytes accessed | tf_op | source)
XLA Modules:
  0.0 75.1 jit_solution(1394154990693128919)
XLA Ops:
  0.6 69.4 %shard_map.175 = (bf16[128,512]{1,0:T(8,128)(2,1)}, bf16[3,128,512]{2,1,0:T(8,128)(2,1)}, f32[128,512]{1,0:T(8,128)}) custom-call(bf16[3,128,512]{2,1,0:T(8,128)(2,1)} %qkv.1, f32[128,512]{1,0:T(8,128)} %filt.1, f32[1,512]{1,0:T(1,128)} %bitcast.1, f32[3,3,512]{2,1,0:T(4,128)} %sw.1, bf16[2048,512]{1,0:T(8,128)(2,1)} %w_out.1, bf16[128,512]{1,0:T(8,128)(2,1)} %g_out.1, ...), custom_call_target="tpu_custom_call" | custom-call | tf_op jit(solution)/shard_map/pallas_call | solution.py:350
  70.1 1.6 %copy.22 = bf16[128,512]{1,0:T(8,128)(2,1)} copy(bf16[128,512]{1,0:T(8,128)(2,1)} %get-tuple-element.6) | data formatting | bytes 262144
  71.7 1.8 %copy.23 = bf16[3,128,512]{2,1,0:T(8,128)(2,1)} copy(bf16[3,128,512]{2,1,0:T(8,128)(2,1)} %get-tuple-element.7) | data formatting | bytes 786432
  73.4 1.7 %copy.24 = f32[128,512]{1,0:T(8,128)} copy(f32[128,512]{1,0:T(8,128)} %get-tuple-element.8) | data formatting | bytes 524288

commit v3 on v2

--- a/solution.py
+++ b/solution.py
@@ -13,8 +13,11 @@
 F32 = jnp.float32
 MESH = pl.DeviceIdType.MESH
 Z_CHIPS = 16
-OWN = 4
-FILT, MIXED, GRAD, CONV, CORR, GFIL = range(6)
+VMEM_LIMIT = 67043328
+HALVES = 2
+OWN = 2
+FILT, MIXED, GRAD, CONV, CORR, GFIL = (HALVES * i for i in range(6))
+UNITS = 6 * HALVES
 
 
 def split_const(a):
@@ -24,7 +27,8 @@
 
 def dft_tables(blocks, rows, z_chips):
     q = np.arange(blocks)
-    yc, z = q // z_chips, q % z_chips
+    lines = blocks // z_chips
+    z, yc = q // lines, q % lines
     p = ((yc // 2) * z_chips + z) * 2 + yc % 2
     c = np.arange(blocks)[:, None] + 0.5
     outer = 2 * np.pi * p[None, :] * c / (2 * blocks)
@@ -54,16 +58,21 @@
     return high, (a - high.astype(F32)).astype(BF16)
 
 
-def kernel(
-    shape,
-    qkv, filt, skip, sw, w_out, g_out,
-    ah, al, bh, bl, mh, ml, uh, ul, tcos, tsin,
+def kernel(shape, *refs):
+    inputs, results = refs[:16], refs[16:19]
+    kept, loaded = refs[19:35], refs[35]
+    body(shape, inputs, kept, loaded, *results, *refs[36:])
+
+
+def body(
+    shape, inputs, kept, loaded,
     output, grad_qkv, grad_filter,
     send, mid, recv, halo, ghalo_out, ghalo_in, part_out, part_in, gate_out, gate_in,
     xs, ext, spec, gs, shorts, gg, glong,
     send1, recv1, send2, recv2, loc1, loc2, hsem, psend, precv, gsend, grecv,
 ):
     blocks, zn, slabs, rows, width = shape
+    qkv, filt, skip, sw, w_out, g_out, ah, al, bh, bl, mh, ml, uh, ul, tcos, tsin = kept
     lines = blocks // zn
     s = lax.axis_index("seq")
     ch = lax.axis_index("ch")
@@ -104,6 +113,15 @@
     greet(after, ch)
     greet(before, ch)
 
+    loads = [
+        pltpu.make_async_copy(src, dst, loaded.at[i])
+        for i, (src, dst) in enumerate(zip(inputs, kept))
+    ]
+    for i in (5, 4, 1, 0, 3, 2):
+        loads[i].start()
+    for copy in loads[6:]:
+        copy.start()
+
     def slab(k):
         return w_out[pl.ds(pl.multiple_of(k * width, width), width), :]
 
@@ -112,23 +130,28 @@
             g_out[...], slab(k), (((1,), (1,)), ((), ())), preferred_element_type=F32
         )
 
+    group = width // HALVES
+
+    def columns(h):
+        return pl.ds(h * group, group)
+
     def pack(u, value):
-        send[u] = jnp.swapaxes(value, 0, 1).astype(BF16).reshape(lines, zn, OWN, rows)
+        send[u] = jnp.swapaxes(value, 0, 1).astype(BF16).reshape(zn, lines, OWN, rows)
 
     def unpack(u):
-        return jnp.swapaxes(recv[u].astype(F32).reshape(width, rows), 0, 1)
+        return jnp.swapaxes(recv[u].astype(F32).reshape(group, rows), 0, 1)
 
     def own1(u):
-        return pltpu.make_async_copy(send.at[u, :, z], mid.at[u, z], loc1.at[u])
+        return pltpu.make_async_copy(send.at[u, z], mid.at[u, z], loc1.at[u])
 
     def own2(u):
-        return pltpu.make_async_copy(mid.at[u, :, yc], recv.at[u, yc], loc2.at[u])
+        return pltpu.make_async_copy(mid.at[u, :, yc], recv.at[u, :, yc], loc2.at[u])
 
     def start1(u):
         def go(i, _):
             other, device = on_z(i)
             pltpu.make_async_remote_copy(
-                src_ref=send.at[u, :, other],
+                src_ref=send.at[u, other],
                 dst_ref=mid.at[u, z],
                 send_sem=send1.at[u],
                 recv_sem=recv1.at[u],
@@ -149,7 +172,7 @@
             other, device = on_line(i)
             pltpu.make_async_remote_copy(
                 src_ref=mid.at[u, :, other],
-                dst_ref=recv.at[u, yc],
+                dst_ref=recv.at[u, :, yc],
                 send_sem=send2.at[u],
                 recv_sem=recv2.at[u],
                 device_id=(device, ch),
@@ -162,13 +185,13 @@
 
     def finish(u):
         own2(u).wait()
-        landed = recv.at[u, pl.ds(0, lines - 1)]
+        landed = recv.at[u, :, pl.ds(0, lines - 1)]
         pltpu.make_async_copy(landed, landed, recv2.at[u]).wait()
 
     def drain(u):
         sent = mid.at[u, pl.ds(0, zn - 1)]
         pltpu.make_async_copy(sent, sent, send1.at[u]).wait()
-        sent = recv.at[u, pl.ds(0, lines - 1)]
+        sent = recv.at[u, :, pl.ds(0, lines - 1)]
         pltpu.make_async_copy(sent, sent, send2.at[u]).wait()
 
     def to_slab(i, k, src, dst, ssem, rsem):
@@ -207,7 +230,7 @@
     ]
 
     def ahead(u, k):
-        xs[...] = recv[u].astype(F32).reshape(width, rows)
+        xs[...] = recv[u].astype(F32).reshape(group, rows)
         x = jnp.concatenate(
             [xs[pl.ds(j, blocks, stride=OWN), :] for j in range(OWN)], axis=1
         ).astype(BF16)
@@ -234,21 +257,45 @@
         t = dot(bh[...], high) + dot(bl[...], high) + dot(bh[...], low)
         for j in range(OWN):
             xs[pl.ds(j, blocks, stride=OWN), :] = t[:, j * rows : (j + 1) * rows]
-        send[u] = xs[...].astype(BF16).reshape(lines, zn, OWN, rows)
-
+        send[u] = xs[...].astype(BF16).reshape(zn, lines, OWN, rows)
+
+    def spectra(k, h):
+        k = k + h
+        return spec[k, :, :rows], spec[k, :, rows:]
+
+    def convolve(h):
+        (mre, mim), (fre, fim) = spectra(MIXED, h), spectra(FILT, h)
+        back(CONV + h, mre * fre - mim * fim, mre * fim + mim * fre)
+        start1(CONV + h)
+
+    def correlate(u, k, h):
+        (are, aim), (gre, gim) = spectra(k, h), spectra(GRAD, h)
+        back(u + h, are * gre + aim * gim, are * gim - aim * gre)
+        start1(u + h)
+
+    def land(u):
+        finish(u)
+        ahead(u, u)
+
+    loads[5].wait()
+    loads[4].wait()
     for i in range(slabs - 1):
         part_out[i] = rows_of((ch + i + 1) % slabs).astype(BF16)
-    pack(FILT, filt[...])
+    loads[1].wait()
+    for h in range(HALVES):
+        pack(FILT + h, filt[:, columns(h)])
     gg[...] = rows_of(ch)
+    for i in (0, 3, 2):
+        loads[i].wait()
     pl.semaphore_wait(barrier, zn - 1 + lines - 1 + slabs - 1 + 2)
 
     halo_copy.start()
+    start1(FILT)
     for copy in part_copies:
         copy.start()
-    start1(FILT)
 
     halo_copy.wait_recv()
-    for i in range(3):
+    for i in (1, 2, 0):
         head = halo[i].astype(F32)
         ext[pl.ds(0, 8), :] = jnp.where(s > 0, head, jnp.zeros_like(head))
         ext[pl.ds(8, rows), :] = qkv[i].astype(F32)
@@ -257,8 +304,12 @@
             + sw[i, pl.ds(1, 1), :] * ext[pl.ds(7, rows), :]
             + sw[i, pl.ds(2, 1), :] * ext[pl.ds(6, rows), :]
         )
-    pack(MIXED, shorts[1] * shorts[2])
-    start1(MIXED)
+        if i == 2:
+            for h in range(HALVES):
+                pack(MIXED + h, shorts[1, :, columns(h)] * shorts[2, :, columns(h)])
+                start1(MIXED + h)
+                if h + 1 < HALVES:
+                    start1(FILT + h + 1)
 
     total = gg[...]
     for i in range(slabs - 1):
@@ -266,57 +317,70 @@
         total = total + part_in[i].astype(F32)
     gg[...] = total
     glong[...] = total * shorts[0]
-    pack(GRAD, glong[...])
-    start1(GRAD)
+    for h in range(HALVES):
+        pack(GRAD + h, glong[:, columns(h)])
+        start1(GRAD + h)
 
     start2(FILT)
     start2(MIXED)
-    finish(FILT)
-    ahead(FILT, 0)
-    finish(MIXED)
-    ahead(MIXED, 1)
-
-    fre, fim = spec[0, :, :rows], spec[0, :, rows:]
-    mre, mim = spec[1, :, :rows], spec[1, :, rows:]
-    back(CONV, mre * fre - mim * fim, mre * fim + mim * fre)
-    start1(CONV)
+    for copy in loads[6:]:
+        copy.wait()
+    land(FILT)
+    start2(FILT + 1)
+    land(MIXED)
+    convolve(0)
+    start2(MIXED + 1)
+    land(FILT + 1)
     start2(GRAD)
-    finish(GRAD)
-    ahead(GRAD, 2)
-    fre, fim = spec[0, :, :rows], spec[0, :, rows:]
-    gre, gim = spec[2, :, :rows], spec[2, :, rows:]
-    back(CORR, fre * gre + fim * gim, fre * gim - fim * gre)
-    start1(CORR)
+    land(MIXED + 1)
+    convolve(1)
+    start2(GRAD + 1)
+    land(GRAD)
+    correlate(CORR, FILT, 0)
+    correlate(GFIL, MIXED, 0)
     start2(CONV)
-    mre, mim = spec[1, :, :rows], spec[1, :, rows:]
-    gre, gim = spec[2, :, :rows], spec[2, :, rows:]
-    back(GFIL, mre * gre + mim * gim, mre * gim - mim * gre)
-    start1(GFIL)
-
-    finish(CONV)
-    long_out = unpack(CONV) + skip[...] * (shorts[1] * shorts[2])
-    gate_out[...] = (shorts[0] * long_out).astype(BF16)
+    land(GRAD + 1)
+    correlate(CORR, FILT, 1)
+    correlate(GFIL, MIXED, 1)
+    start2(CONV + 1)
+    start2(CORR)
+
+    for h in range(HALVES):
+        finish(CONV + h)
+        at = columns(h)
+        mixed = shorts[1, :, at] * shorts[2, :, at]
+        long_out = unpack(CONV + h) + skip[:, at] * mixed
+        gate_out[:, at] = (shorts[0, :, at] * long_out).astype(BF16)
+        gs[0, :, at] = gg[:, at] * long_out
     for copy in gate_copies:
         copy.start()
-    gs[0] = gg[...] * long_out
-
-    start2(CORR)
     total = dot(gate_out[...], slab(ch))
+
+    start2(GFIL)
+
+    def mix_grads(h):
+        finish(CORR + h)
+        at = columns(h)
+        grad_mixed = unpack(CORR + h) + skip[:, at] * glong[:, at]
+        gs[1, :, at] = grad_mixed * shorts[2, :, at]
+        gs[2, :, at] = grad_mixed * shorts[1, :, at]
+
+    def filter_grads(h):
+        finish(GFIL + h)
+        grad_filter[:, columns(h)] = unpack(GFIL + h) * (1.0 / math.sqrt(blocks * rows))
+
+    mix_grads(0)
+    start2(CORR + 1)
+    filter_grads(0)
+    start2(GFIL + 1)
+    mix_grads(1)
+    ghalo_out[...] = gs[:, pl.ds(0, 8), :]
+    ghalo_copy.start()
+
     for i in range(slabs - 1):
         gate_copies[i].wait_recv()
         total = total + dot(gate_in[i], slab((ch + slabs - 1 - i) % slabs))
     output[...] = total.astype(BF16)
-
-    start2(GFIL)
-    finish(CORR)
-    grad_mixed = unpack(CORR) + skip[...] * glong[...]
-    gs[1] = grad_mixed * shorts[2]
-    gs[2] = grad_mixed * shorts[1]
-    ghalo_out[...] = gs[:, pl.ds(0, 8), :]
-    ghalo_copy.start()
-
-    finish(GFIL)
-    grad_filter[...] = unpack(GFIL) * (1.0 / math.sqrt(blocks * rows))
 
     ghalo_copy.wait_recv()
     for i in range(3):
@@ -328,13 +392,27 @@
             + sw[i, pl.ds(1, 1), :] * ext[pl.ds(1, rows), :]
             + sw[i, pl.ds(2, 1), :] * ext[pl.ds(2, rows), :]
         ).astype(BF16)
+    filter_grads(1)
 
     halo_copy.wait_send()
     ghalo_copy.wait_send()
     for copy in part_copies + gate_copies:
         copy.wait_send()
-    for u in range(6):
+    for u in range(UNITS):
         drain(u)
+
+
+def write_out(*refs):
+    ins, outs, held, sem = refs[:3], refs[3:6], refs[6:9], refs[9]
+    pulls = [pltpu.make_async_copy(ins[i], held[i], sem.at[i]) for i in range(3)]
+    pushes = [pltpu.make_async_copy(held[i], outs[i], sem.at[i + 3]) for i in range(3)]
+    for copy in pulls:
+        copy.start()
+    for pull, push in zip(pulls, pushes):
+        pull.wait()
+        push.start()
+    for copy in pushes:
+        copy.wait()
 
 
 def local(qkv, filt, skip_gain, short_weight, w_out, g_out):
@@ -344,21 +422,24 @@
     zn = Z_CHIPS
     lines = blocks // zn
     tables = dft_tables(blocks, rows, zn)
+    args = (qkv, filt, skip_gain[None, :], short_weight, w_out, g_out, *tables)
     vmem = pl.BlockSpec(memory_space=pltpu.VMEM)
-    unit = (6, lines, zn, OWN, rows)
+    unit = (UNITS, zn, lines, OWN, rows)
     dma = pltpu.SemaphoreType.DMA
-    return pl.pallas_call(
+    results = pl.pallas_call(
         functools.partial(kernel, (blocks, zn, slabs, rows, width)),
         out_shape=(
             jax.ShapeDtypeStruct((rows, width), BF16),
             jax.ShapeDtypeStruct((3, rows, width), BF16),
             jax.ShapeDtypeStruct((rows, width), F32),
         ),
-        in_specs=[vmem] * (6 + len(tables)),
+        in_specs=[pl.BlockSpec(memory_space=pltpu.HBM)] * len(args),
         out_specs=(vmem, vmem, vmem),
         scratch_shapes=[
+            *[pltpu.VMEM(a.shape, a.dtype) for a in args],
+            dma((len(args),)),
             pltpu.VMEM(unit, BF16),
-            pltpu.VMEM((6, zn, lines, OWN, rows), BF16),
+            pltpu.VMEM(unit, BF16),
             pltpu.VMEM(unit, BF16),
             pltpu.VMEM((3, 8, width), BF16),
             pltpu.VMEM((3, 8, width), F32),
@@ -367,19 +448,29 @@
             pltpu.VMEM((slabs - 1, rows, width), BF16),
             pltpu.VMEM((rows, width), BF16),
             pltpu.VMEM((slabs - 1, rows, width), BF16),
-            pltpu.VMEM((width, rows), F32),
+            pltpu.VMEM((OWN * blocks, rows), F32),
             pltpu.VMEM((rows + 8, width), F32),
-            pltpu.VMEM((3, OWN * blocks, 2 * rows), F32),
+            pltpu.VMEM((3 * HALVES, OWN * blocks, 2 * rows), F32),
             pltpu.VMEM((3, rows, width), F32),
             pltpu.VMEM((3, rows, width), F32),
             pltpu.VMEM((rows, width), F32),
             pltpu.VMEM((rows, width), F32),
-            dma((6,)), dma((6,)), dma((6,)), dma((6,)), dma((6,)), dma((6,)),
+            *[dma((UNITS,))] * 6,
             dma((4,)),
             dma((slabs - 1,)), dma((slabs - 1,)), dma((slabs - 1,)), dma((slabs - 1,)),
         ],
-        compiler_params=pltpu.CompilerParams(collective_id=0, has_side_effects=True),
-    )(qkv, filt, skip_gain[None, :], short_weight, w_out, g_out, *tables)
+        compiler_params=pltpu.CompilerParams(
+            collective_id=0, has_side_effects=True, vmem_limit_bytes=VMEM_LIMIT
+        ),
+    )(*args)
+    return pl.pallas_call(
+        write_out,
+        out_shape=tuple(jax.ShapeDtypeStruct(r.shape, r.dtype) for r in results),
+        in_specs=[pl.BlockSpec(memory_space=pltpu.HBM)] * 3,
+        out_specs=[pl.BlockSpec(memory_space=pltpu.HBM)] * 3,
+        scratch_shapes=[*[pltpu.VMEM(r.shape, r.dtype) for r in results], dma((6,))],
+        compiler_params=pltpu.CompilerParams(vmem_limit_bytes=VMEM_LIMIT),
+    )(*results)
 
 
 def solution(mesh):

time: 75.3 us -> 65 us (0.86)
  Pallas kernels: 69.4 us -> 64.2 us
  local copies, waits for them, and re-layouts: 5 us -> 0 us
    pallas_call x1, Pallas kernels: 69.4 us -> 62.3 us  [local(): pl.pallas_call(functools.partial(kernel, (blocks, zn, slabs, rows, width)...]
    unnamed x3 -> x0, local copies, waits for them, and re-layouts: 5 us -> none
    pallas_call x0 -> x1, Pallas kernels: none -> 1.95 us  [local(): pl.pallas_call(write_out, out_shape=tuple((jax.ShapeDtypeStruct(r.shape,...]
where the time goes in v3:
time: 65 us; the launch traced here: 64.9 us
  Pallas kernels  64.2 us (99%)
    pallas_call x1, Pallas kernels, local(): pl.pallas_call(functools.partial(kernel, (blocks, zn, slabs, rows, width)...  62.3 us
    pallas_call x1, Pallas kernels, local(): pl.pallas_call(write_out, out_shape=tuple((jax.ShapeDtypeStruct(r.shape,...  1.95 us

profile of v3, /device:TPU:1, one launch (start us, length us, event | category | flops | bytes accessed | tf_op | source)
XLA Modules:
  0.0 64.9 jit_solution(9096732144127912276)
XLA Ops:
  0.6 62.3 %shard_map.175 = (bf16[128,512]{1,0:T(8,128)(2,1)}, bf16[3,128,512]{2,1,0:T(8,128)(2,1)}, f32[128,512]{1,0:T(8,128)}) custom-call(bf16[3,128,512]{2,1,0:T(8,128)(2,1)} %refs_0_.1, f32[128,512]{1,0:T(8,128)} %refs_1_.1, f32[1,512]{1,0:T(1,128)} %bitcast.1, f32[3,3,512]{2,1,0:T(4,128)} %refs_3_.1, bf16[2048,512]{1,0:T(8,128)(2,1)} %refs_4_.1, ...), custom_call_target="tpu_custom_call" | custom-call | tf_op jit(solution)/shard_map/pallas_call | solution.py:429
  62.9 2.0 %shard_map.176 = (bf16[128,512]{1,0:T(8,128)(2,1)}, bf16[3,128,512]{2,1,0:T(8,128)(2,1)}, f32[128,512]{1,0:T(8,128)}) custom-call(bf16[128,512]{1,0:T(8,128)(2,1)} %get-tuple-element.6.refs_0_, bf16[3,128,512]{2,1,0:T(8,128)(2,1)} %get-tuple-element.7.refs_1_, f32[128,512]{1,0:T(8,128)} %get-tuple-element.8.refs_2_), custom_call_target="tpu_custom_call" | custom-call | tf_op jit(solution)/shard_map/pallas_call | solution.py:466

commit v4 on v3

--- a/solution.py
+++ b/solution.py
@@ -18,6 +18,7 @@
 OWN = 2
 FILT, MIXED, GRAD, CONV, CORR, GFIL = (HALVES * i for i in range(6))
 UNITS = 6 * HALVES
+LINE_FIRST = (FILT + 1, MIXED + 1, GRAD, GRAD + 1, CORR + 1, GFIL, GFIL + 1)
 
 
 def split_const(a):
@@ -141,65 +142,69 @@
     def unpack(u):
         return jnp.swapaxes(recv[u].astype(F32).reshape(group, rows), 0, 1)
 
-    def own1(u):
-        return pltpu.make_async_copy(send.at[u, z], mid.at[u, z], loc1.at[u])
-
-    def own2(u):
-        return pltpu.make_async_copy(mid.at[u, :, yc], recv.at[u, :, yc], loc2.at[u])
-
-    def start1(u):
+    def on_lines(u, src, dst, ssem, rsem, lsem):
         def go(i, _):
-            other, device = on_z(i)
+            other, device = on_line(i)
             pltpu.make_async_remote_copy(
-                src_ref=send.at[u, other],
-                dst_ref=mid.at[u, z],
-                send_sem=send1.at[u],
-                recv_sem=recv1.at[u],
+                src_ref=src.at[u, :, other],
+                dst_ref=dst.at[u, :, yc],
+                send_sem=ssem.at[u],
+                recv_sem=rsem.at[u],
                 device_id=(device, ch),
                 device_id_type=MESH,
             ).start()
             return 0
 
-        lax.fori_loop(0, zn - 1, go, 0)
-        own1(u).start()
-
-    def start2(u):
-        own1(u).wait()
-        landed = mid.at[u, pl.ds(0, zn - 1)]
-        pltpu.make_async_copy(landed, landed, recv1.at[u]).wait()
-
+        lax.fori_loop(0, lines - 1, go, 0)
+        pltpu.make_async_copy(src.at[u, :, yc], dst.at[u, :, yc], lsem.at[u]).start()
+
+    def on_zs(u, src, dst, ssem, rsem, lsem):
         def go(i, _):
-            other, device = on_line(i)
+            other, device = on_z(i)
             pltpu.make_async_remote_copy(
-                src_ref=mid.at[u, :, other],
-                dst_ref=recv.at[u, :, yc],
-                send_sem=send2.at[u],
-                recv_sem=recv2.at[u],
+                src_ref=src.at[u, other],
+                dst_ref=dst.at[u, z],
+                send_sem=ssem.at[u],
+                recv_sem=rsem.at[u],
                 device_id=(device, ch),
                 device_id_type=MESH,
             ).start()
             return 0
 
-        lax.fori_loop(0, lines - 1, go, 0)
-        own2(u).start()
+        lax.fori_loop(0, zn - 1, go, 0)
+        pltpu.make_async_copy(src.at[u, z], dst.at[u, z], lsem.at[u]).start()
+
+    def moved(u, buf, by_line, sem):
+        part = buf.at[u, :, pl.ds(0, lines - 1)] if by_line else buf.at[u, pl.ds(0, zn - 1)]
+        pltpu.make_async_copy(part, part, sem.at[u]).wait()
+
+    def arrived(u, buf, by_line, rsem, lsem):
+        own = buf.at[u, :, yc] if by_line else buf.at[u, z]
+        pltpu.make_async_copy(own, own, lsem.at[u]).wait()
+        moved(u, buf, by_line, rsem)
+
+    def first(u):
+        go = on_lines if u in LINE_FIRST else on_zs
+        go(u, send, mid, send1, recv1, loc1)
+
+    def second(u):
+        arrived(u, mid, u in LINE_FIRST, recv1, loc1)
+        go = on_zs if u in LINE_FIRST else on_lines
+        go(u, mid, recv, send2, recv2, loc2)
 
     def finish(u):
-        own2(u).wait()
-        landed = recv.at[u, :, pl.ds(0, lines - 1)]
-        pltpu.make_async_copy(landed, landed, recv2.at[u]).wait()
+        arrived(u, recv, u not in LINE_FIRST, recv2, loc2)
 
     def drain(u):
-        sent = mid.at[u, pl.ds(0, zn - 1)]
-        pltpu.make_async_copy(sent, sent, send1.at[u]).wait()
-        sent = recv.at[u, :, pl.ds(0, lines - 1)]
-        pltpu.make_async_copy(sent, sent, send2.at[u]).wait()
+        moved(u, mid, u in LINE_FIRST, send1)
+        moved(u, recv, u not in LINE_FIRST, send2)
 
     def to_slab(i, k, src, dst, ssem, rsem):
         return pltpu.make_async_remote_copy(
             src_ref=src,
             dst_ref=dst,
-            send_sem=ssem.at[i],
-            recv_sem=rsem.at[i],
+            send_sem=ssem.at[*i],
+            recv_sem=rsem.at[*i],
             device_id=(s, k),
             device_id_type=MESH,
         )
@@ -220,13 +225,20 @@
         device_id=(before, ch),
         device_id_type=MESH,
     )
+    others = range(slabs - 1)
     part_copies = [
-        to_slab(i, (ch + i + 1) % slabs, part_out.at[i], part_in.at[i], psend, precv)
-        for i in range(slabs - 1)
+        [
+            to_slab((h, i), (ch + i + 1) % slabs, part_out.at[h, i], part_in.at[h, i], psend, precv)
+            for i in others
+        ]
+        for h in range(HALVES)
     ]
     gate_copies = [
-        to_slab(i, (ch + i + 1) % slabs, gate_out, gate_in.at[i], gsend, grecv)
-        for i in range(slabs - 1)
+        [
+            to_slab((h, i), (ch + i + 1) % slabs, gate_out.at[h], gate_in.at[h, i], gsend, grecv)
+            for i in others
+        ]
+        for h in range(HALVES)
     ]
 
     def ahead(u, k):
@@ -266,12 +278,12 @@
     def convolve(h):
         (mre, mim), (fre, fim) = spectra(MIXED, h), spectra(FILT, h)
         back(CONV + h, mre * fre - mim * fim, mre * fim + mim * fre)
-        start1(CONV + h)
+        first(CONV + h)
 
     def correlate(u, k, h):
         (are, aim), (gre, gim) = spectra(k, h), spectra(GRAD, h)
         back(u + h, are * gre + aim * gim, are * gim - aim * gre)
-        start1(u + h)
+        first(u + h)
 
     def land(u):
         finish(u)
@@ -279,8 +291,10 @@
 
     loads[5].wait()
     loads[4].wait()
-    for i in range(slabs - 1):
-        part_out[i] = rows_of((ch + i + 1) % slabs).astype(BF16)
+    for i in others:
+        part = rows_of((ch + i + 1) % slabs).astype(BF16)
+        for h in range(HALVES):
+            part_out[h, i] = part[:, h * group : (h + 1) * group]
     loads[1].wait()
     for h in range(HALVES):
         pack(FILT + h, filt[:, columns(h)])
@@ -290,12 +304,13 @@
     pl.semaphore_wait(barrier, zn - 1 + lines - 1 + slabs - 1 + 2)
 
     halo_copy.start()
-    start1(FILT)
-    for copy in part_copies:
-        copy.start()
-
-    halo_copy.wait_recv()
-    for i in (1, 2, 0):
+    first(FILT)
+    first(FILT + 1)
+    for copies in part_copies:
+        for copy in copies:
+            copy.start()
+
+    def shorten(i):
         head = halo[i].astype(F32)
         ext[pl.ds(0, 8), :] = jnp.where(s > 0, head, jnp.zeros_like(head))
         ext[pl.ds(8, rows), :] = qkv[i].astype(F32)
@@ -304,59 +319,63 @@
             + sw[i, pl.ds(1, 1), :] * ext[pl.ds(7, rows), :]
             + sw[i, pl.ds(2, 1), :] * ext[pl.ds(6, rows), :]
         )
-        if i == 2:
-            for h in range(HALVES):
-                pack(MIXED + h, shorts[1, :, columns(h)] * shorts[2, :, columns(h)])
-                start1(MIXED + h)
-                if h + 1 < HALVES:
-                    start1(FILT + h + 1)
-
-    total = gg[...]
-    for i in range(slabs - 1):
-        part_copies[i].wait_recv()
-        total = total + part_in[i].astype(F32)
-    gg[...] = total
-    glong[...] = total * shorts[0]
+
+    halo_copy.wait_recv()
+    shorten(1)
+    shorten(2)
     for h in range(HALVES):
-        pack(GRAD + h, glong[:, columns(h)])
-        start1(GRAD + h)
-
-    start2(FILT)
-    start2(MIXED)
+        pack(MIXED + h, shorts[1, :, columns(h)] * shorts[2, :, columns(h)])
+        first(MIXED + h)
+    second(FILT + 1)
+    shorten(0)
+
+    def long_grads(h):
+        at = columns(h)
+        total = gg[:, at]
+        for i in others:
+            part_copies[h][i].wait_recv()
+            total = total + part_in[h, i].astype(F32)
+        gg[:, at] = total
+        glong[:, at] = total * shorts[0, :, at]
+        pack(GRAD + h, glong[:, at])
+        first(GRAD + h)
+
+    long_grads(0)
+    second(MIXED + 1)
+    long_grads(1)
+    second(FILT)
+    second(GRAD)
+    second(GRAD + 1)
+    second(MIXED)
     for copy in loads[6:]:
         copy.wait()
     land(FILT)
-    start2(FILT + 1)
+    land(FILT + 1)
     land(MIXED)
     convolve(0)
-    start2(MIXED + 1)
-    land(FILT + 1)
-    start2(GRAD)
     land(MIXED + 1)
     convolve(1)
-    start2(GRAD + 1)
     land(GRAD)
     correlate(CORR, FILT, 0)
     correlate(GFIL, MIXED, 0)
-    start2(CONV)
     land(GRAD + 1)
     correlate(CORR, FILT, 1)
+    second(GFIL)
     correlate(GFIL, MIXED, 1)
-    start2(CONV + 1)
-    start2(CORR)
-
-    for h in range(HALVES):
+    second(CONV)
+    second(CORR + 1)
+    second(GFIL + 1)
+    second(CONV + 1)
+
+    def gate(h):
         finish(CONV + h)
         at = columns(h)
         mixed = shorts[1, :, at] * shorts[2, :, at]
         long_out = unpack(CONV + h) + skip[:, at] * mixed
-        gate_out[:, at] = (shorts[0, :, at] * long_out).astype(BF16)
+        gate_out[h] = (shorts[0, :, at] * long_out).astype(BF16)
+        for copy in gate_copies[h]:
+            copy.start()
         gs[0, :, at] = gg[:, at] * long_out
-    for copy in gate_copies:
-        copy.start()
-    total = dot(gate_out[...], slab(ch))
-
-    start2(GFIL)
 
     def mix_grads(h):
         finish(CORR + h)
@@ -369,17 +388,26 @@
         finish(GFIL + h)
         grad_filter[:, columns(h)] = unpack(GFIL + h) * (1.0 / math.sqrt(blocks * rows))
 
+    def half_slab(k, h):
+        start = pl.multiple_of(k * width + h * group, group)
+        return w_out[pl.ds(start, group), :]
+
+    gate(0)
+    second(CORR)
+    gate(1)
+    total = dot(gate_out[0], half_slab(ch, 0))
+    for h in range(1, HALVES):
+        total = total + dot(gate_out[h], half_slab(ch, h))
+    filter_grads(0)
     mix_grads(0)
-    start2(CORR + 1)
-    filter_grads(0)
-    start2(GFIL + 1)
     mix_grads(1)
     ghalo_out[...] = gs[:, pl.ds(0, 8), :]
     ghalo_copy.start()
 
-    for i in range(slabs - 1):
-        gate_copies[i].wait_recv()
-        total = total + dot(gate_in[i], slab((ch + slabs - 1 - i) % slabs))
+    for h in range(HALVES):
+        for i in others:
+            gate_copies[h][i].wait_recv()
+            total = total + dot(gate_in[h, i], half_slab((ch + slabs - 1 - i) % slabs, h))
     output[...] = total.astype(BF16)
 
     ghalo_copy.wait_recv()
@@ -396,8 +424,9 @@
 
     halo_copy.wait_send()
     ghalo_copy.wait_send()
-    for copy in part_copies + gate_copies:
-        copy.wait_send()
+    for copies in part_copies + gate_copies:
+        for copy in copies:
+            copy.wait_send()
     for u in range(UNITS):
         drain(u)
 
@@ -444,10 +473,10 @@
             pltpu.VMEM((3, 8, width), BF16),
             pltpu.VMEM((3, 8, width), F32),
             pltpu.VMEM((3, 8, width), F32),
-            pltpu.VMEM((slabs - 1, rows, width), BF16),
-            pltpu.VMEM((slabs - 1, rows, width), BF16),
-            pltpu.VMEM((rows, width), BF16),
-            pltpu.VMEM((slabs - 1, rows, width), BF16),
+            pltpu.VMEM((HALVES, slabs - 1, rows, width // HALVES), BF16),
+            pltpu.VMEM((HALVES, slabs - 1, rows, width // HALVES), BF16),
+            pltpu.VMEM((HALVES, rows, width // HALVES), BF16),
+            pltpu.VMEM((HALVES, slabs - 1, rows, width // HALVES), BF16),
             pltpu.VMEM((OWN * blocks, rows), F32),
             pltpu.VMEM((rows + 8, width), F32),
             pltpu.VMEM((3 * HALVES, OWN * blocks, 2 * rows), F32),
@@ -457,7 +486,7 @@
             pltpu.VMEM((rows, width), F32),
             *[dma((UNITS,))] * 6,
             dma((4,)),
-            dma((slabs - 1,)), dma((slabs - 1,)), dma((slabs - 1,)), dma((slabs - 1,)),
+            *[dma((HALVES, slabs - 1))] * 4,
         ],
         compiler_params=pltpu.CompilerParams(
             collective_id=0, has_side_effects=True, vmem_limit_bytes=VMEM_LIMIT

time: 65 us -> 61.2 us (0.942)
  Pallas kernels: 64.2 us -> 60.4 us
    pallas_call x1, Pallas kernels: 62.3 us -> 58.5 us  [local(): pl.pallas_call(functools.partial(kernel, (blocks, zn, slabs, rows, width)...]
where the time goes in v4:
time: 61.2 us; the launch traced here: 61.1 us
  Pallas kernels  60.4 us (99%)
  between operations  0.64 us (1%)
    pallas_call x1, Pallas kernels, local(): pl.pallas_call(functools.partial(kernel, (blocks, zn, slabs, rows, width)...  58.5 us
    pallas_call x1, Pallas kernels, local(): pl.pallas_call(write_out, out_shape=tuple((jax.ShapeDtypeStruct(r.shape,...  1.95 us

profile of v4, /device:TPU:1, one launch (start us, length us, event | category | flops | bytes accessed | tf_op | source)
XLA Modules:
  0.0 61.1 jit_solution(13611638827721036948)
XLA Ops:
  0.6 58.5 %shard_map.175 = (bf16[128,512]{1,0:T(8,128)(2,1)}, bf16[3,128,512]{2,1,0:T(8,128)(2,1)}, f32[128,512]{1,0:T(8,128)}) custom-call(bf16[3,128,512]{2,1,0:T(8,128)(2,1)} %refs_0_.1, f32[128,512]{1,0:T(8,128)} %refs_1_.1, f32[1,512]{1,0:T(1,128)} %bitcast.1, f32[3,3,512]{2,1,0:T(4,128)} %refs_3_.1, bf16[2048,512]{1,0:T(8,128)(2,1)} %refs_4_.1, ...), custom_call_target="tpu_custom_call" | custom-call | tf_op jit(solution)/shard_map/pallas_call | solution.py:458
  59.1 2.0 %shard_map.176 = (bf16[128,512]{1,0:T(8,128)(2,1)}, bf16[3,128,512]{2,1,0:T(8,128)(2,1)}, f32[128,512]{1,0:T(8,128)}) custom-call(bf16[128,512]{1,0:T(8,128)(2,1)} %get-tuple-element.6.refs_0_, bf16[3,128,512]{2,1,0:T(8,128)(2,1)} %get-tuple-element.7.refs_1_, f32[128,512]{1,0:T(8,128)} %get-tuple-element.8.refs_2_), custom_call_target="tpu_custom_call" | custom-call | tf_op jit(solution)/shard_map/pallas_call | solution.py:495

commit v5 on v4

--- a/solution.py
+++ b/solution.py
@@ -13,7 +13,7 @@
 F32 = jnp.float32
 MESH = pl.DeviceIdType.MESH
 Z_CHIPS = 16
-VMEM_LIMIT = 67043328
+VMEM_LIMIT = 32 * 1024 * 1024
 HALVES = 2
 OWN = 2
 FILT, MIXED, GRAD, CONV, CORR, GFIL = (HALVES * i for i in range(6))
@@ -432,15 +432,11 @@
 
 
 def write_out(*refs):
-    ins, outs, held, sem = refs[:3], refs[3:6], refs[6:9], refs[9]
-    pulls = [pltpu.make_async_copy(ins[i], held[i], sem.at[i]) for i in range(3)]
-    pushes = [pltpu.make_async_copy(held[i], outs[i], sem.at[i + 3]) for i in range(3)]
-    for copy in pulls:
+    sem = refs[6]
+    copies = [pltpu.make_async_copy(refs[i], refs[3 + i], sem.at[i]) for i in range(3)]
+    for copy in copies:
         copy.start()
-    for pull, push in zip(pulls, pushes):
-        pull.wait()
-        push.start()
-    for copy in pushes:
+    for copy in copies:
         copy.wait()
 
 
@@ -458,9 +454,9 @@
     results = pl.pallas_call(
         functools.partial(kernel, (blocks, zn, slabs, rows, width)),
         out_shape=(
-            jax.ShapeDtypeStruct((rows, width), BF16),
-            jax.ShapeDtypeStruct((3, rows, width), BF16),
-            jax.ShapeDtypeStruct((rows, width), F32),
+            pltpu.VMEM((rows, width), BF16),
+            pltpu.VMEM((3, rows, width), BF16),
+            pltpu.VMEM((rows, width), F32),
         ),
         in_specs=[pl.BlockSpec(memory_space=pltpu.HBM)] * len(args),
         out_specs=(vmem, vmem, vmem),
@@ -491,13 +487,13 @@
         compiler_params=pltpu.CompilerParams(
             collective_id=0, has_side_effects=True, vmem_limit_bytes=VMEM_LIMIT
         ),
-    )(*args)
+    )(*(pltpu.with_memory_space_constraint(a, pltpu.HBM) for a in args))
     return pl.pallas_call(
         write_out,
         out_shape=tuple(jax.ShapeDtypeStruct(r.shape, r.dtype) for r in results),
-        in_specs=[pl.BlockSpec(memory_space=pltpu.HBM)] * 3,
+        in_specs=[vmem] * 3,
         out_specs=[pl.BlockSpec(memory_space=pltpu.HBM)] * 3,
-        scratch_shapes=[*[pltpu.VMEM(r.shape, r.dtype) for r in results], dma((6,))],
+        scratch_shapes=[dma((3,))],
         compiler_params=pltpu.CompilerParams(vmem_limit_bytes=VMEM_LIMIT),
     )(*results)
 

time: 61.2 us -> 59.3 us (0.969)
  Pallas kernels: 60.4 us -> 58.5 us
    pallas_call x1, Pallas kernels: 1.95 us -> 0.9 us  [local(): pl.pallas_call(write_out, out_shape=tuple((jax.ShapeDtypeStruct(r.shape,...]
    pallas_call x1, Pallas kernels: 58.5 us -> 57.6 us  [local(): pl.pallas_call(functools.partial(kernel, (blocks, zn, slabs, rows, width)...]
where the time goes in v5:
time: 59.3 us; the launch traced here: 59.2 us
  Pallas kernels  58.5 us (99%)
  between operations  0.64 us (1%)
    pallas_call x1, Pallas kernels, local(): pl.pallas_call(functools.partial(kernel, (blocks, zn, slabs, rows, width)...  57.6 us

profile of v5, /device:TPU:1, one launch (start us, length us, event | category | flops | bytes accessed | tf_op | source)
XLA Modules:
  0.0 59.2 jit_solution(1229421981304147157)
XLA Ops:
  0.6 57.6 %shard_map.175 = (bf16[128,512]{1,0:T(8,128)(2,1)S(1)}, bf16[3,128,512]{2,1,0:T(8,128)(2,1)S(1)}, f32[128,512]{1,0:T(8,128)S(1)}) custom-call(bf16[3,128,512]{2,1,0:T(8,128)(2,1)} %refs_0_.1, f32[128,512]{1,0:T(8,128)} %refs_1_.1, f32[1,512]{1,0:T(1,128)} %bitcast.1, f32[3,3,512]{2,1,0:T(4,128)} %refs_3_.1, bf16[2048,512]{1,0:T(8,128)(2,1)} %refs_4_.1, ...), custom_call_target="tpu_custom_call" | custom-call | tf_op jit(solution)/shard_map/pallas_call | solution.py:454
  58.3 0.9 %shard_map.176 = (bf16[128,512]{1,0:T(8,128)(2,1)}, bf16[3,128,512]{2,1,0:T(8,128)(2,1)}, f32[128,512]{1,0:T(8,128)}) custom-call(bf16[128,512]{1,0:T(8,128)(2,1)S(1)} %get-tuple-element.6.refs_0_, bf16[3,128,512]{2,1,0:T(8,128)(2,1)S(1)} %get-tuple-element.7.refs_1_, f32[128,512]{1,0:T(8,128)S(1)} %get-tuple-element.8.refs_2_), custom_call_target="tpu_custom_call" | custom-call | tf_op jit(solution)/shard_map/pallas_call | solution.py:491

commit v6 on v5

--- a/solution.py
+++ b/solution.py
@@ -70,7 +70,7 @@
     output, grad_qkv, grad_filter,
     send, mid, recv, halo, ghalo_out, ghalo_in, part_out, part_in, gate_out, gate_in,
     xs, ext, spec, gs, shorts, gg, glong,
-    send1, recv1, send2, recv2, loc1, loc2, hsem, psend, precv, gsend, grecv,
+    send1, recv1, send2, recv2, loc1, loc2, hsem, psend, precv, gsend, grecv, met_sem,
 ):
     blocks, zn, slabs, rows, width = shape
     qkv, filt, skip, sw, w_out, g_out, ah, al, bh, bl, mh, ml, uh, ul, tcos, tsin = kept
@@ -99,26 +99,38 @@
     def greet(a, b):
         pl.semaphore_signal(barrier, inc=1, device_id=(a, b), device_id_type=MESH)
 
-    def greet_z(i, _):
-        greet(on_z(i)[1], ch)
-        return 0
+    def on_ring(dz):
+        return (y * zn + (z + dz) % zn) * 2 + core
 
     def greet_line(i, _):
         greet(on_line(i)[1], ch)
         return 0
 
-    lax.fori_loop(0, zn - 1, greet_z, 0)
+    strides = [2**j for j in range(zn.bit_length() - 2)]
+    near = sorted({1, zn - 1})
+    for dz in near:
+        greet(on_ring(dz), ch)
     lax.fori_loop(0, lines - 1, greet_line, 0)
     for i in range(1, slabs):
         greet(s, (ch + i) % slabs)
     greet(after, ch)
     greet(before, ch)
 
+    def meet(j):
+        for side, dz in enumerate((strides[j], zn - strides[j])):
+            pl.semaphore_signal(
+                met_sem.at[j, side], inc=1, device_id=(on_ring(dz), ch), device_id_type=MESH
+            )
+
+    def met(j):
+        for side in range(2):
+            pl.semaphore_wait(met_sem.at[j, side], 1)
+
     loads = [
         pltpu.make_async_copy(src, dst, loaded.at[i])
         for i, (src, dst) in enumerate(zip(inputs, kept))
     ]
-    for i in (5, 4, 1, 0, 3, 2):
+    for i in (0, 1, 5, 4, 3, 2):
         loads[i].start()
     for copy in loads[6:]:
         copy.start()
@@ -158,7 +170,9 @@
         lax.fori_loop(0, lines - 1, go, 0)
         pltpu.make_async_copy(src.at[u, :, yc], dst.at[u, :, yc], lsem.at[u]).start()
 
-    def on_zs(u, src, dst, ssem, rsem, lsem):
+    distant = zn // 2 - 1
+
+    def on_zs(u, src, dst, ssem, rsem, lsem, which=""):
         def go(i, _):
             other, device = on_z(i)
             pltpu.make_async_remote_copy(
@@ -171,8 +185,9 @@
             ).start()
             return 0
 
-        lax.fori_loop(0, zn - 1, go, 0)
-        pltpu.make_async_copy(src.at[u, z], dst.at[u, z], lsem.at[u]).start()
+        lax.fori_loop(distant if which == "near" else 0, distant if which == "far" else zn - 1, go, 0)
+        if which != "far":
+            pltpu.make_async_copy(src.at[u, z], dst.at[u, z], lsem.at[u]).start()
 
     def moved(u, buf, by_line, sem):
         part = buf.at[u, :, pl.ds(0, lines - 1)] if by_line else buf.at[u, pl.ds(0, zn - 1)]
@@ -186,6 +201,14 @@
     def first(u):
         go = on_lines if u in LINE_FIRST else on_zs
         go(u, send, mid, send1, recv1, loc1)
+
+    def first_part(u, which):
+        on_zs(u, send, mid, send1, recv1, loc1, which)
+
+    def second_part(u, which):
+        if which == "near":
+            arrived(u, mid, True, recv1, loc1)
+        on_zs(u, mid, recv, send2, recv2, loc2, which)
 
     def second(u):
         arrived(u, mid, u in LINE_FIRST, recv1, loc1)
@@ -289,26 +312,11 @@
         finish(u)
         ahead(u, u)
 
-    loads[5].wait()
-    loads[4].wait()
-    for i in others:
+    def partial_grads(i):
         part = rows_of((ch + i + 1) % slabs).astype(BF16)
         for h in range(HALVES):
             part_out[h, i] = part[:, h * group : (h + 1) * group]
-    loads[1].wait()
-    for h in range(HALVES):
-        pack(FILT + h, filt[:, columns(h)])
-    gg[...] = rows_of(ch)
-    for i in (0, 3, 2):
-        loads[i].wait()
-    pl.semaphore_wait(barrier, zn - 1 + lines - 1 + slabs - 1 + 2)
-
-    halo_copy.start()
-    first(FILT)
-    first(FILT + 1)
-    for copies in part_copies:
-        for copy in copies:
-            copy.start()
+            part_copies[h][i].start()
 
     def shorten(i):
         head = halo[i].astype(F32)
@@ -320,13 +328,48 @@
             + sw[i, pl.ds(2, 1), :] * ext[pl.ds(6, rows), :]
         )
 
+    steps = len(strides)
+    loads[0].wait()
+    pl.semaphore_wait(barrier, len(near) + lines - 1 + slabs - 1 + 2)
+    if steps:
+        meet(0)
+    halo_copy.start()
+    loads[1].wait()
+    for h in reversed(range(HALVES)):
+        pack(FILT + h, filt[:, columns(h)])
+        if h:
+            first(FILT + h)
+    if steps > 2:
+        met(0)
+        meet(1)
+    loads[5].wait()
+    loads[4].wait()
+    partial_grads(0)
+    if steps > 1:
+        met(steps - 2)
+        meet(steps - 1)
+    first_part(FILT, "near")
+    for i in range(1, slabs - 1):
+        partial_grads(i)
+    second_part(FILT + 1, "near")
+
     halo_copy.wait_recv()
+    loads[3].wait()
+    loads[2].wait()
     shorten(1)
     shorten(2)
     for h in range(HALVES):
         pack(MIXED + h, shorts[1, :, columns(h)] * shorts[2, :, columns(h)])
-        first(MIXED + h)
-    second(FILT + 1)
+        if h:
+            first(MIXED + h)
+        else:
+            first_part(MIXED, "near")
+    if steps:
+        met(steps - 1)
+    first_part(FILT, "far")
+    first_part(MIXED, "far")
+    second_part(FILT + 1, "far")
+    gg[...] = rows_of(ch)
     shorten(0)
 
     def long_grads(h):
@@ -483,6 +526,7 @@
             *[dma((UNITS,))] * 6,
             dma((4,)),
             *[dma((HALVES, slabs - 1))] * 4,
+            pltpu.SemaphoreType.REGULAR((3, 2)),
         ],
         compiler_params=pltpu.CompilerParams(
             collective_id=0, has_side_effects=True, vmem_limit_bytes=VMEM_LIMIT

time: 59.3 us -> 61.4 us (1.035)
  Pallas kernels: 58.5 us -> 60.6 us
    pallas_call x1, Pallas kernels: 57.6 us -> 59.7 us  [local(): pl.pallas_call(functools.partial(kernel, (blocks, zn, slabs, rows, width)...]
where the time goes in v6:
time: 61.4 us; the launch traced here: 61.2 us
  Pallas kernels  60.6 us (99%)
  between operations  0.64 us (1%)
    pallas_call x1, Pallas kernels, local(): pl.pallas_call(functools.partial(kernel, (blocks, zn, slabs, rows, width)...  59.7 us

profile of v6, /device:TPU:1, one launch (start us, length us, event | category | flops | bytes accessed | tf_op | source)
XLA Modules:
  0.0 61.2 jit_solution(12376672277858396475)
XLA Ops:
  0.6 59.7 %shard_map.175 = (bf16[128,512]{1,0:T(8,128)(2,1)S(1)}, bf16[3,128,512]{2,1,0:T(8,128)(2,1)S(1)}, f32[128,512]{1,0:T(8,128)S(1)}) custom-call(bf16[3,128,512]{2,1,0:T(8,128)(2,1)} %refs_0_.1, f32[128,512]{1,0:T(8,128)} %refs_1_.1, f32[1,512]{1,0:T(1,128)} %bitcast.1, f32[3,3,512]{2,1,0:T(4,128)} %refs_3_.1, bf16[2048,512]{1,0:T(8,128)(2,1)} %refs_4_.1, ...), custom_call_target="tpu_custom_call" | custom-call | tf_op jit(solution)/shard_map/pallas_call | solution.py:497
  60.3 0.9 %shard_map.176 = (bf16[128,512]{1,0:T(8,128)(2,1)}, bf16[3,128,512]{2,1,0:T(8,128)(2,1)}, f32[128,512]{1,0:T(8,128)}) custom-call(bf16[128,512]{1,0:T(8,128)(2,1)S(1)} %get-tuple-element.6.refs_0_, bf16[3,128,512]{2,1,0:T(8,128)(2,1)S(1)} %get-tuple-element.7.refs_1_, f32[128,512]{1,0:T(8,128)S(1)} %get-tuple-element.8.refs_2_), custom_call_target="tpu_custom_call" | custom-call | tf_op jit(solution)/shard_map/pallas_call | solution.py:535

commit v7 on v5

--- a/solution.py
+++ b/solution.py
@@ -303,12 +303,14 @@
         loads[i].wait()
     pl.semaphore_wait(barrier, zn - 1 + lines - 1 + slabs - 1 + 2)
 
+    for copy in part_copies[0]:
+        copy.start()
     halo_copy.start()
     first(FILT)
-    first(FILT + 1)
-    for copies in part_copies:
+    for copies in part_copies[1:]:
         for copy in copies:
             copy.start()
+    first(FILT + 1)
 
     def shorten(i):
         head = halo[i].astype(F32)

time: 59.3 us -> 59.1 us (level)
  no operation moved by 1% of the time
where the time goes in v7:
time: 59.1 us; the launch traced here: 59 us
  Pallas kernels  58.3 us (99%)
  between operations  0.64 us (1%)
    pallas_call x1, Pallas kernels, local(): pl.pallas_call(functools.partial(kernel, (blocks, zn, slabs, rows, width)...  57.4 us

profile of v7, /device:TPU:1, one launch (start us, length us, event | category | flops | bytes accessed | tf_op | source)
XLA Modules:
  0.0 59.0 jit_solution(10239754983123882716)
XLA Ops:
  0.6 57.4 %shard_map.175 = (bf16[128,512]{1,0:T(8,128)(2,1)S(1)}, bf16[3,128,512]{2,1,0:T(8,128)(2,1)S(1)}, f32[128,512]{1,0:T(8,128)S(1)}) custom-call(bf16[3,128,512]{2,1,0:T(8,128)(2,1)} %refs_0_.1, f32[128,512]{1,0:T(8,128)} %refs_1_.1, f32[1,512]{1,0:T(1,128)} %bitcast.1, f32[3,3,512]{2,1,0:T(4,128)} %refs_3_.1, bf16[2048,512]{1,0:T(8,128)(2,1)} %refs_4_.1, ...), custom_call_target="tpu_custom_call" | custom-call | tf_op jit(solution)/shard_map/pallas_call | solution.py:456
  58.1 0.9 %shard_map.176 = (bf16[128,512]{1,0:T(8,128)(2,1)}, bf16[3,128,512]{2,1,0:T(8,128)(2,1)}, f32[128,512]{1,0:T(8,128)}) custom-call(bf16[128,512]{1,0:T(8,128)(2,1)S(1)} %get-tuple-element.6.refs_0_, bf16[3,128,512]{2,1,0:T(8,128)(2,1)S(1)} %get-tuple-element.7.refs_1_, f32[128,512]{1,0:T(8,128)S(1)} %get-tuple-element.8.refs_2_), custom_call_target="tpu_custom_call" | custom-call | tf_op jit(solution)/shard_map/pallas_call | solution.py:493
